TPU v7x, 256 devices: a whole 4x4x8 slice. The times are simulated.
256 devices in a mesh: tm: 64 (over z_hi, y, x), freq: 4 (over z_lo, core).
Axes of the slice: x: 4, y: 4, z: 8 (z_hi: 4, z_lo: 2; z = z_hi * 2 + z_lo), core: 2. Of those that a mesh axis runs over, the one named last changes fastest.
Arguments:
- spectrum: bfloat16 [1024, 49152], P('freq', 'tm'), may hold values from 0.0099487305 to 10
- decay_rate: float32 [1024], P('freq'), may hold values from 1e-07 to 0.03
- init_state: float32 [1024], P('freq'), may hold values from 0.3 to 3
- clip_ids: int32 [49152], P('tm'), may hold values from 0 to 5, never falling along the last dimension, each value on 1 to 16384 neighbouring positions
- encoder: bfloat16 [256, 1024], P(None, 'freq'), may hold values from -0.1875 to 0.1875
- gauss_noise: float32 [256, 49152], P(None, 'tm'), may hold values from -3 to 3
- uniform_noise: float32 [2, 256, 49152], P(None, None, 'tm'), may hold values from 0.02 to 1
- boost_count: int32 [256], replicated, may hold values from 1 to 2
- templates: bfloat16 [1024, 4096], P('freq'), may hold values from 0.0099487305 to 1
Outputs:
- frame_loss: float32 [49152], P('tm')
- template_grad: float32 [4096, 1024], P('tm', 'freq')
Inputs may be any that keep to these rules, and one draw needn't show every extreme that they name: `clip_ids`: clip numbers never fall along the frames; each clip holds 1 to 16384 frames, one exactly that many.
All inputs are finite; a program needn't handle non-finite values.
Results may differ from a plain program's by a relative error of at most 0.00033.
Values may be sent and summed in bfloat16 or wider, within the bound.
A program may use at most 64 MiB of HBM per device.

v0:
```python
import jax
import jax.numpy as jnp
from jax import lax
from jax.sharding import PartitionSpec as P

F = 1024
K = 256
L = 16


def prefix(part, axis, combine, identity):
    place = lax.axis_index(axis)
    gathered = jax.tree.map(lambda a: lax.all_gather(a, axis), part)
    state = jax.tree.map(lambda a, e: jnp.zeros_like(a) + jnp.asarray(e, a.dtype), part, identity)

    def one(lap, state):
        return combine(
            state, jax.tree.map(lambda a: lax.dynamic_index_in_dim(a, lap, 0, False), gathered)
        )

    return lax.fori_loop(0, place, one, state)


def passed_along(value, axis, steps):
    count = lax.axis_size(axis)
    leading, last = (max(0, -steps), min(count, count - steps))
    return lax.ppermute(value, axis, [(source, source + steps) for source in range(leading, last)])


def compose(former, latter):
    return (former[0] * latter[0], latter[0] * former[1] + latter[1])


def linked(former, latter):
    p_one, q_one, first_one, last_one, start_one, mark_one = former
    p_two, q_two, first_two, last_two, start_two, mark_two = latter
    joined = (last_one >= 0.0) & (first_two >= 0.0) & (first_two != last_one)
    factor = jnp.where(joined, 0.8, 1.0)
    scaled = p_two * factor
    merged_p = scaled * p_one
    merged_q = scaled * q_one + q_two
    first_clip = jnp.where(first_one >= 0.0, first_one, first_two)
    start_frame = jnp.where(first_one >= 0.0, start_one, start_two)
    last_clip = jnp.where(last_two >= 0.0, last_two, last_one)
    latest = jnp.maximum(jnp.maximum(mark_one, jnp.where(joined, start_two, -1.0)), mark_two)
    return (merged_p, merged_q, first_clip, last_clip, start_frame, latest)


def topic_mixture(logits, gaussian, uniforms, boost_count):
    concentration = jax.nn.softplus(logits) + 0.5
    boosted = boost_count[:, None]
    shape_total = concentration + boosted.astype(jnp.float32)
    offset = shape_total - 1.0 / 3.0
    spread = lax.rsqrt(9.0 * offset)
    linear = 1.0 + spread * gaussian
    gamma_draw = offset * linear * linear * linear * jnp.exp(jnp.log(uniforms[0]) / concentration)
    gamma_draw = gamma_draw * jnp.where(
        boosted >= 2, jnp.exp(jnp.log(uniforms[1]) / (concentration + 1.0)), 1.0
    )
    return (gamma_draw / jnp.sum(gamma_draw, axis=0, keepdims=True)).astype(jnp.bfloat16)


def on_device(
    spectrum,
    decay_rate,
    init_state,
    clip_ids,
    encoder,
    gauss_noise,
    uniform_noise,
    boost_count,
    templates,
):
    frames = spectrum.shape[1]
    bins = spectrum.shape[0]
    rim_width = L - 1
    spectral = spectrum.astype(jnp.float32)
    changed = clip_ids[1:] != clip_ids[:-1]
    factor_row = jnp.concatenate(
        [jnp.ones((1,), jnp.float32), jnp.where(changed, 0.8, 1.0).astype(jnp.float32)]
    )
    rates = (1.0 - decay_rate)[:, None] * factor_row[None, :]
    inputs = decay_rate[:, None] * spectral
    running, summed = lax.associative_scan(compose, (rates, inputs), axis=1)
    anchor = lax.axis_index("tm") * frames
    positions = anchor + jnp.arange(frames, dtype=jnp.int32)
    marks = jnp.where(jnp.concatenate([jnp.zeros((1,), bool), changed]), positions, -1)
    clip_float = clip_ids.astype(jnp.float32)
    summary = (
        running[:, -1],
        summed[:, -1],
        clip_float[:1],
        clip_float[-1:],
        jnp.reshape(anchor.astype(jnp.float32), (1,)),
        jnp.reshape(jnp.max(marks).astype(jnp.float32), (1,)),
    )
    minus_one = jnp.full((1,), -1.0, jnp.float32)
    identity_tuple = (
        jnp.ones((bins,), jnp.float32),
        jnp.zeros((bins,), jnp.float32),
        minus_one,
        minus_one,
        minus_one,
        minus_one,
    )
    before = prefix(summary, "tm", linked, identity_tuple)
    junction = (before[3] >= 0.0) & (clip_float[:1] != before[3])
    entry = jnp.where(junction, 0.8, 1.0) * (before[0] * init_state + before[1])
    smooth = running * entry[:, None] + summed
    normed = (spectral * lax.rsqrt(smooth + 0.1)).astype(jnp.bfloat16)
    code_part = jnp.dot(encoder, normed, preferred_element_type=jnp.float32)
    logits = lax.psum(code_part, "freq")
    proportions = topic_mixture(logits, gauss_noise, uniform_noise, boost_count)
    topics = proportions.shape[0]
    rim = passed_along(proportions[:, frames - rim_width :], "tm", 1)
    extended = jnp.concatenate([rim, proportions], axis=1)
    flags = jnp.concatenate([junction, changed]).astype(jnp.int32)
    clean = jnp.cumsum(flags) == 0
    clip_pad = jnp.concatenate([jnp.full((rim_width,), -1, jnp.int32), clip_ids])
    lag_rows = []
    mask_rows = []
    for lag in range(L):
        begin = rim_width - lag
        lag_rows.append(extended[:, begin : begin + frames])
        source = jnp.arange(frames, dtype=jnp.int32) - lag
        same_clip = clip_pad[begin : begin + frames] == clip_ids
        earlier = clean & (before[5] <= (anchor + source).astype(jnp.float32))
        mask_rows.append(jnp.where(source >= 0, same_clip, earlier))
    valid = jnp.stack(mask_rows).astype(jnp.bfloat16)
    stacked = (jnp.stack(lag_rows, axis=1) * valid[None]).reshape(topics * L, frames)
    recon = jnp.dot(templates, stacked, preferred_element_type=jnp.float32)
    sums_part = (
        jnp.sum(recon, axis=0),
        jnp.sum(spectral, axis=0),
        jnp.sum(spectral * jnp.log(recon), axis=0),
    )
    recon_sum, spec_sum, log_sum = lax.psum((sums_part[0], sums_part[1], sums_part[2]), "freq")
    frame_loss = jnp.log(recon_sum) - log_sum / spec_sum
    scale_factor = F * K / (frames * lax.axis_size("tm"))
    ratio = (
        scale_factor * (1.0 / recon_sum[None, :] - spectral / (spec_sum[None, :] * recon))
    ).astype(jnp.bfloat16)
    owned_rows = topics * L // lax.axis_size("tm")
    full_grad = lax.dot_general(
        stacked, ratio, (((1,), (1,)), ((), ())), preferred_element_type=jnp.float32
    )
    total_grad = lax.psum(full_grad, "tm")
    template_grad = lax.dynamic_slice_in_dim(
        total_grad, lax.axis_index("tm") * owned_rows, owned_rows, 0
    )
    return (frame_loss, template_grad)


def solution(mesh):
    placed = (
        P("freq", "tm"),
        P("freq"),
        P("freq"),
        P("tm"),
        P(None, "freq"),
        P(None, "tm"),
        P(None, None, "tm"),
        P(),
        P("freq", None),
    )
    return jax.shard_map(
        on_device, mesh=mesh, in_specs=placed, out_specs=(P("tm"), P("tm", "freq")), check_vma=False
    )
```

profile of v0, /device:TPU:32, one launch (start us, length us, event | category | flops | bytes accessed | tf_op | source)
XLA Modules:
  0.0 1997.5 jit_solution(15807336264710183670)
XLA Ops:
  17.0 3.1 slice.440
  20.2 3.2 slice.439
  23.3 2.3 fusion.127
  98.1 3.2 slice.480
  121.8 2.5 pad.144
  129.5 2.3 add_multiply_fusion.1
  133.7 2.9 pad.128
  137.3 193.9 %all-gather = f32[16384,1]{0,1:T(1,128)S(1)} all-gather(f32[256,1]{0,1:T(1,128)S(1)} %slice_add_fusion.3), channel_id=2, replica_groups=mesh['tm'=64,'freq'=4] {'tm'}, dimensions={0}, use_global_device_ids=true | all-gather | bytes 66560 | tf_op jit(solution)/shard_map/all_gather | solution.py:13
  341.2 2.9 pad.145
  344.0 2.8 pad.146
  347.6 183.9 %all-gather.2 = f32[16384,1]{0,1:T(1,128)S(1)} all-gather(f32[256,1]{0,1:T(1,128)S(1)} %slice_add_fusion), channel_id=4, replica_groups=mesh['tm'=64,'freq'=4] {'tm'}, dimensions={0}, use_global_device_ids=true | all-gather | bytes 66560 | tf_op jit(solution)/shard_map/all_gather | solution.py:13
  534.4 188.1 %all-reduce.41 = (f32[64]{0:T(128)S(1)}, f32[64]{0:T(128)S(1)}, f32[64]{0:T(128)S(1)}, f32[64]{0:T(128)S(1)}) all-reduce(f32[64]{0:T(128)S(1)} %get-tuple-element.234, f32[64]{0:T(128)} %copy-done.6, f32[64]{0:T(128)S(1)} %dynamic-update-slice.2, f32[64]{0:T(128)S(1)} %dynamic-update-slice.3), channel_id=3, replica_groups=mesh['tm'=64,'freq'=4] {'tm'}, use_global_device_ids=true, to_apply=%add.37 | all-reduce | flops 256 | bytes 2048
  724.0 3.0 convolution_bitcast_fusion
  727.0 2.3 fusion.126
  729.3 2.3 copy.87
  734.9 440.1 %all-reduce.46.cloned.1.call-done = f32[256,768]{0,1:T(8,128)} async-done(((f32[256,768]{0,1:T(8,128)}), f32[256,768]{0,1:T(8,128)}) %all-reduce.46.cloned.1.call-update) | async-done | bytes 786448 | tf_op jit(solution)/shard_map/psum | solution.py:112
  1175.0 2.8 fusion.124
  1178.7 3.7 collective-permute-start
  1196.2 7.2 broadcast_multiply_fusion
  1203.4 9.0 copy.83
  1212.4 5.5 fusion.136
  1219.6 10.4 all-reduce.42
  1230.7 6.8 fusion.11
  1237.5 751.7 %all-reduce.48.cloned.1.call-done = f32[4096,256]{1,0:T(8,128)} async-done(((f32[4096,256]{1,0:T(8,128)}), f32[4096,256]{1,0:T(8,128)}) %all-reduce.48.cloned.1.call-update) | async-done | bytes 4194320 | tf_op jit(solution)/shard_map/psum | solution.py:147
  (237 shorter events, 145.5 us)
Async XLA Ops:
  7.2 1205.3 %copy-start = (bf16[256,4096]{1,0:T(8,128)(2,1)S(1)}, bf16[256,4096]{1,0:T(8,128)(2,1)}, u32[]{:S(2)}) copy-start(bf16[256,4096]{1,0:T(8,128)(2,1)} %param.19) | copy-start | bytes 6291460
  7.2 1167.8 %all-reduce.46.cloned.1.call-start = ((), (), s32[]{:S(2)}) async-start(), calls=%async_computation | async-start | bytes 1572864 | tf_op jit(solution)/shard_map/psum | solution.py:112
  9.6 92.4 %copy-start.1 = (f32[256,768]{0,1:T(8,128)}, f32[256,768]{0,1:T(8,128)S(1)}, u32[]{:S(2)}) copy-start(f32[256,768]{0,1:T(8,128)S(1)} %broadcast_multiply_fusion.1) | copy-start | bytes 2359300
  15.4 86.6 %copy-start.3 = (s32[768]{0:T(1024)S(1)}, s32[768]{0:T(1024)}, u32[]{:S(2)}) copy-start(s32[768]{0:T(1024)} %param.14) | copy-start | bytes 9220
  113.3 18.5 slice-start
  119.8 218.1 %copy-start.4 = (pred[767]{0:T(1024)(128)(4,1)S(1)}, pred[767]{0:T(1024)(128)(4,1)}, u32[]{:S(2)}) copy-start(pred[767]{0:T(1024)(128)(4,1)} %get-tuple-element.180) | copy-start | bytes 2305
  119.8 219.6 %slice-start.1 = ((f32[256,768]{0,1:T(8,128)}), f32[256,1]{0,1:T(1,128)S(1)}, s32[]{:S(2)}) async-start(f32[256,768]{0,1:T(8,128)} %convert_multiply_fusion.2), calls=%async_computation.3 | async-start | bytes 2048 | tf_op jit(solution)/shard_map/slice | solution.py:84
  128.7 595.3 %copy-start.2 = (bf16[256,256]{1,0:T(8,128)(2,1)S(1)}, bf16[256,256]{1,0:T(8,128)(2,1)}, u32[]{:S(2)}) copy-start(bf16[256,256]{1,0:T(8,128)(2,1)} %param.15) | copy-start | bytes 393220
  337.9 9.0 copy-start.6
  724.0 10.2 copy-start.5
  726.9 1262.2 %all-reduce.48.cloned.1.call-start = ((), (), s32[]{:S(2)}) async-start(), calls=%async_computation.1 | async-start | bytes 8388608 | tf_op jit(solution)/shard_map/psum | solution.py:147
  1178.7 4.9 collective-permute-start
Sparse Core Ops, SparseCore 0:
  727.1 447.8 all-reduce.45
  1237.6 751.4 all-reduce.47
where the time goes:
time: 2010 us; the launch traced here: 2000 us
  waiting for transfers between devices  1190 us (59%)
  blocking collectives  576 us (29%)
  local copies, waits for them, and re-layouts  124 us (6%)
  other arithmetic  69.7 us (3%)
    psum x1, waiting for transfers between devices, on_device(): total_grad = lax.psum(full_grad, 'tm')  752 us
    psum x1, waiting for transfers between devices, on_device(): logits = lax.psum(code_part, 'freq')  440 us
    all_gather x2, blocking collectives, prefix(): gathered = jax.tree.map(lambda a: lax.all_gather(a, axis), part)  378 us
    unnamed x1, blocking collectives  188 us
    slice x66, local copies, waits for them, and re-layouts, on_device(): running, summed = lax.associative_scan(compose, (rates, inputs), axis=1)  77.9 us
  transfers between devices with their start and end apart: 3, of which 3 were waited for; matrix products, arithmetic and copies ran while one was open for 0% of the time, Pallas kernels for 0%

commit v1 on v0

v1 whole, which is shorter than its diff:
```python
import jax
import jax.numpy as jnp
from jax import lax
from jax.experimental import pallas as pl
from jax.experimental.pallas import tpu as pltpu
from jax.sharding import PartitionSpec as P

F = 1024
K = 256
L = 16
TIME = 49152
BINS = 256
FRAMES = 768
TILES = 6
TM = 64
NF = 4
MESH = pl.DeviceIdType.MESH
f32 = jnp.float32
bf16 = jnp.bfloat16
LOG_GAIN = 0.22314355131420976
OWNER = (0, 0, 1, 2, 2, 3)
SLOT = (0, 1, 0, 0, 1, 0)


def remote(src, dst, send, recv, tm, fq):
    return pltpu.make_async_remote_copy(
        src_ref=src, dst_ref=dst, send_sem=send, recv_sem=recv,
        device_id={"tm": tm, "freq": fq}, device_id_type=MESH,
    )


def kernel(
    spec_ref, decay_ref, init_ref, ids_ref, enc_ref, boost_ref, gauss_hbm, unif_hbm, tmpl_hbm,
    loss_ref, out_ref,
    tmpl, gbuf, ubuf, encf, grow, cum, normed, nbuf, pbuf, pf, idh, qsend, qbuf, st,
    recon, sbuf, rat, grad, a1, c3, r1, r2, r3,
    load_sem, enc_s, enc_r, q_s, q_r, id_s, id_r, n_s, n_r, p_s, p_r, h_s, h_r, s_s, s_r,
    rs1_s, rs1_r, rs2_s, rs2_r, rs3_s, rs3_r,
):
    tm = lax.axis_index("tm")
    fq = lax.axis_index("freq")
    core = lax.rem(fq, 2)
    zlo = fq // 2
    barrier = pltpu.get_barrier_semaphore()
    nxt = lax.rem(tm + 1, TM)
    prv = lax.rem(tm + TM - 1, TM)

    def greet(i, carry):
        pl.semaphore_signal(
            barrier, inc=1, device_id={"tm": lax.rem(tm + i, TM), "freq": fq}, device_id_type=MESH)
        return carry

    lax.fori_loop(1, TM, greet, 0)
    for i in range(1, NF):
        other = lax.rem(fq + i, NF)
        for place in (tm, nxt, prv):
            pl.semaphore_signal(
                barrier, inc=1, device_id={"tm": place, "freq": other}, device_id_type=MESH)

    first = zlo * 3 + core * 2
    load_t = pltpu.make_async_copy(tmpl_hbm, tmpl, load_sem.at[0])
    load_t.start()

    def tile_loads(slot):
        cols = pl.ds(pl.multiple_of((first + slot) * 128, 128), 128)
        return (
            pltpu.make_async_copy(gauss_hbm.at[:, cols], gbuf.at[slot], load_sem.at[1 + 2 * slot]),
            pltpu.make_async_copy(unif_hbm.at[:, :, cols], ubuf.at[slot], load_sem.at[2 + 2 * slot]),
        )

    for copy in tile_loads(0):
        copy.start()

    @pl.when(core == 0)
    def _():
        for copy in tile_loads(1):
            copy.start()

    rows = lax.broadcasted_iota(jnp.int32, (BINS, BINS), 0)
    cols = lax.broadcasted_iota(jnp.int32, (BINS, BINS), 1)
    eye = rows == cols
    tri = (rows <= cols).astype(bf16)

    def column(row):
        return jnp.sum(jnp.where(eye, jnp.broadcast_to(row, (BINS, BINS)), 0.0), axis=1, keepdims=True)

    def row_of(col):
        return jnp.sum(jnp.where(eye, jnp.broadcast_to(col, (BINS, BINS)), 0.0), axis=0, keepdims=True)

    decay_row = decay_ref[...]
    lost = 1.0 - (1.0 - decay_row)
    log_row = -lost * (1.0 + lost * (1 / 2 + lost * (1 / 3 + lost * (1 / 4 + lost * (1 / 5 + lost * (1 / 6))))))
    log_col = column(log_row)
    decay_col = column(decay_row)
    ids = ids_ref[...].astype(f32)
    lift = jnp.exp(ids * LOG_GAIN)
    carry = jnp.zeros((BINS, 1), f32)
    for b in range(3):
        span = slice(b * 256, b * 256 + 256)
        steps = (cols + (b * 256 + 1)).astype(f32)
        power = steps * log_col
        grow[:, span] = jnp.exp(power)
        v = decay_col * (spec_ref[:, span].astype(f32) * lift[:, span]) * jnp.exp(-power)
        hi = v.astype(bf16)
        rest = v - hi.astype(f32)
        mid = rest.astype(bf16)
        low = (rest - mid.astype(f32)).astype(bf16)
        c = (
            jnp.dot(hi, tri, preferred_element_type=f32)
            + jnp.dot(mid, tri, preferred_element_type=f32)
            + jnp.dot(low, tri, preferred_element_type=f32)
        ) + carry
        cum[:, span] = c
        carry = c[:, 255:256]
    q_col = carry * jnp.exp(log_col * float(FRAMES))
    qsend[...] = row_of(q_col)

    pl.semaphore_wait(barrier, TM - 1 + 3 * (NF - 1))

    def q_copy(place):
        return remote(qsend, qbuf.at[tm], q_s.at[place], q_r.at[tm], place, fq)

    def q_start(i, carry):
        q_copy(i).start()
        return carry

    lax.fori_loop(tm + 1, TM, q_start, 0)

    def enc_copy(i):
        return remote(enc_ref, encf.at[fq], enc_s.at[i], enc_r.at[i], tm, lax.rem(fq + i, NF))

    for i in range(1, NF):
        enc_copy(i).start()
    id_copy = remote(ids_ref.at[:, pl.ds(FRAMES - 128, 128)], idh, id_s, id_r, nxt, fq)

    @pl.when(tm < TM - 1)
    def _():
        id_copy.start()

    encf[fq] = enc_ref[...]

    boost = column(boost_ref[...].astype(f32))

    def ready_noise(slot):
        for copy in tile_loads(slot):
            copy.wait()
        ubuf[slot] = jnp.log(ubuf[slot])

    ready_noise(0)

    @pl.when(core == 0)
    def _():
        ready_noise(1)

    def q_wait(j, carry):
        remote(qsend, qbuf.at[j], q_s.at[j], q_r.at[j], tm, fq).wait_recv()
        return carry

    lax.fori_loop(0, tm, q_wait, 0)
    jump = jnp.exp(log_row * float(FRAMES))
    entry = lax.fori_loop(0, tm, lambda j, e: jump * e + qbuf[j], init_ref[...])
    entry_col = column(entry)
    for t in range(TILES):
        span = slice(t * 128, t * 128 + 128)
        drop = jnp.exp(ids[:, span] * (-LOG_GAIN))
        smooth = grow[:, span] * (entry_col + cum[:, span]) * drop
        normed[t] = (spec_ref[:, span].astype(f32) * lax.rsqrt(smooth + 0.1)).astype(bf16)

    def n_copy(t):
        return remote(
            normed.at[t], nbuf.at[SLOT[t], fq], n_s.at[t], n_r.at[SLOT[t], fq], tm, OWNER[t])

    for t in (3, 4, 5, 0, 1, 2):
        @pl.when(fq != OWNER[t])
        def _(t=t):
            n_copy(t).start()

        @pl.when(fq == OWNER[t])
        def _(t=t):
            nbuf[SLOT[t], fq] = normed[t]

    for i in range(1, NF):
        src = lax.rem(fq + NF - i, NF)
        remote(enc_ref, encf.at[src], enc_s.at[i], enc_r.at[i], tm, fq).wait_recv()

    def p_copy(t, i):
        return remote(pbuf.at[1 + t], pbuf.at[1 + t], p_s.at[t, i], p_r.at[t], tm, lax.rem(fq + i, NF))

    def halo_copy(q):
        return remote(pbuf.at[TILES], pbuf.at[0], h_s.at[q], h_r, nxt, q)

    def sample(slot):
        for i in range(1, NF):
            src = lax.rem(fq + i, NF)
            remote(normed.at[0], nbuf.at[slot, src], n_s.at[0], n_r.at[slot, src], tm, fq).wait_recv()
        logits = jnp.dot(encf[0], nbuf[slot, 0], preferred_element_type=f32)
        for q in range(1, NF):
            logits += jnp.dot(encf[q], nbuf[slot, q], preferred_element_type=f32)
        conc = jnp.maximum(logits, 0.0) + jnp.log(1.0 + jnp.exp(-jnp.abs(logits))) + 0.5
        offset = conc + boost - 1.0 / 3.0
        linear = 1.0 + lax.rsqrt(9.0 * offset) * gbuf[slot]
        second = jnp.where(boost >= 1.5, ubuf[slot, 1], 0.0)
        power = ubuf[slot, 0] / conc + second / (conc + 1.0)
        draw = offset * linear * linear * linear * jnp.exp(power)
        total = jnp.sum(draw, axis=0, keepdims=True)
        pbuf[1 + first + slot] = (draw / total).astype(bf16)

    sample(0)
    for t in range(TILES):
        if SLOT[t] == 0:
            @pl.when(fq == OWNER[t])
            def _(t=t):
                for i in range(1, NF):
                    p_copy(t, i).start()

    @pl.when((fq == NF - 1) & (tm < TM - 1))
    def _():
        for q in range(NF):
            halo_copy(q).start()

    @pl.when(core == 0)
    def _():
        sample(1)

    for t in range(TILES):
        if SLOT[t] == 1:
            @pl.when(fq == OWNER[t])
            def _(t=t):
                for i in range(1, NF):
                    p_copy(t, i).start()

    @pl.when(tm == 0)
    def _():
        pbuf[0] = jnp.zeros((K, 128), bf16)
        idh[...] = jnp.full((1, 128), -1, jnp.int32)

    @pl.when(tm > 0)
    def _():
        id_copy.wait_recv()
        halo_copy(0).wait_recv()

    for t in range(TILES):
        @pl.when(fq != OWNER[t])
        def _(t=t):
            p_copy(t, 1).wait_recv()

    lane = lax.broadcasted_iota(jnp.int32, (L, 128), 1)
    lag = lax.broadcasted_iota(jnp.int32, (L, 128), 0)
    head = lane < lag

    def lagged(row):
        return pltpu.roll(jnp.broadcast_to(row, (L, 128)), 0, 1, stride=1, stride_axis=0)

    id_rows = [idh[...].astype(f32)] + [ids[:, t * 128:t * 128 + 128] for t in range(TILES)]
    rolled = [lagged(r) for r in id_rows]
    keep = []
    for t in range(TILES):
        source = jnp.where(head, rolled[t], rolled[t + 1])
        keep.append(source == jnp.broadcast_to(id_rows[t + 1], (L, 128)))

    for t in range(TILES + 1):
        pf[t] = pbuf[t].astype(f32)

    def build_row(k, carry):
        prior = lagged(pf[0, pl.ds(k, 1), :])
        for t in range(TILES):
            current = lagged(pf[t + 1, pl.ds(k, 1), :])
            value = jnp.where(keep[t], jnp.where(head, prior, current), 0.0)
            st[pl.ds(pl.multiple_of(k * L, L), L), t * 128:t * 128 + 128] = value.astype(bf16)
            prior = current
        return carry

    lax.fori_loop(0, K, build_row, 0, unroll=4)

    load_t.wait()
    for b in range(3):
        span = slice(b * 256, b * 256 + 256)
        rec = jnp.dot(tmpl[...], st[:, span], preferred_element_type=f32)
        x = spec_ref[:, span].astype(f32)
        recon[:, span] = x / rec
        sbuf[fq, 0:1, span] = jnp.sum(rec, axis=0, keepdims=True)
        sbuf[fq, 1:2, span] = jnp.sum(x, axis=0, keepdims=True)
        sbuf[fq, 2:3, span] = jnp.sum(x * jnp.log(rec), axis=0, keepdims=True)

    def s_copy(i):
        return remote(sbuf.at[fq], sbuf.at[fq], s_s.at[i], s_r.at[i], tm, lax.rem(fq + i, NF))

    for i in range(1, NF):
        s_copy(i).start()
    for i in range(1, NF):
        src = lax.rem(fq + NF - i, NF)
        remote(sbuf.at[src], sbuf.at[src], s_s.at[i], s_r.at[i], tm, fq).wait_recv()
    sums = sbuf[0, 0:3, :] + sbuf[1, 0:3, :] + sbuf[2, 0:3, :] + sbuf[3, 0:3, :]
    recon_sum, spec_sum, log_sum = sums[0:1], sums[1:2], sums[2:3]
    loss_ref[...] = jnp.log(recon_sum) - log_sum / spec_sum
    scale = F * K / TIME
    plain = scale / recon_sum
    part = scale / spec_sum
    rat[...] = (plain - part * recon[...]).astype(bf16)

    def grads(z, carry):
        g = lax.dot_general(
            st[pl.ds(pl.multiple_of(z * 1024, 1024), 1024), :], rat[...],
            (((1,), (1,)), ((), ())), preferred_element_type=f32)
        g = g.reshape(4, 4, 64, 256)
        grad[0, z] = g[..., 0:128]
        grad[1, z] = g[..., 128:256]
        return carry

    lax.fori_loop(0, 4, grads, 0)

    px = lax.rem(tm, 4)
    py = lax.rem(tm // 4, 4)
    pz = tm // 16

    def along(axis, step):
        if axis == 0:
            return tm - px + lax.rem(px + step, 4)
        if axis == 1:
            return tm - 4 * py + 4 * lax.rem(py + step, 4)
        return tm - 16 * pz + 16 * lax.rem(pz + step, 4)

    class Stage:
        def __init__(self, view, buf, send, recv, axis, pos):
            self.view, self.buf, self.send, self.recv = view, buf, send, recv
            self.right, self.left = along(axis, 1), along(axis, 3)
            self.p1, self.p2, self.p3 = (lax.rem(pos + i, 4) for i in (1, 2, 3))

        def copy(self, n):
            d, h, to = (
                (self.p2, 0, self.right), (self.p1, 1, self.right), (self.p1, 0, self.right),
                (self.p2, 1, self.left), (self.p3, 0, self.left), (self.p3, 1, self.left),
            )[n]
            return remote(
                self.view(d, h), self.buf.at[n], self.send.at[n], self.recv.at[n], to, fq)

        def begin(self):
            for n in (0, 3, 1, 4):
                self.copy(n).start()

        def relay(self):
            self.copy(0).wait_recv()
            v = self.view(self.p1, 0)
            v[...] = v[...] + self.buf[0]
            self.copy(2).start()
            self.copy(3).wait_recv()
            v = self.view(self.p3, 1)
            v[...] = v[...] + self.buf[3]
            self.copy(5).start()

        def finish(self):
            for n in (1, 4, 2, 5):
                self.copy(n).wait_recv()

        def drain(self):
            for n in range(6):
                self.copy(n).wait_send()

    sx = Stage(lambda d, h: grad.at[0, pl.ds(2 * h, 2), :, d], r1.at[0], rs1_s.at[0], rs1_r.at[0], 0, px)
    sy = Stage(lambda d, h: grad.at[1, pl.ds(2 * h, 2), d, :], r1.at[1], rs1_s.at[1], rs1_r.at[1], 1, py)
    sx.begin()
    sy.begin()
    sx.relay()
    sy.relay()
    sx.finish()
    a1[0, 0:2] = grad[0, 0:2, :, px] + r1[0, 2] + r1[0, 4]
    a1[0, 2:4] = grad[0, 2:4, :, px] + r1[0, 1] + r1[0, 5]
    s2 = [
        Stage(lambda d, h: a1.at[0, pl.ds(2 * h, 2), d], r2.at[0], rs2_s.at[0], rs2_r.at[0], 1, py),
        Stage(lambda d, h: a1.at[1, pl.ds(2 * h, 2), d], r2.at[1], rs2_s.at[1], rs2_r.at[1], 0, px),
    ]
    s2[0].begin()
    sy.finish()
    a1[1, 0:2] = grad[1, 0:2, py] + r1[1, 2] + r1[1, 4]
    a1[1, 2:4] = grad[1, 2:4, py] + r1[1, 1] + r1[1, 5]
    s2[1].begin()
    s2[0].relay()
    s2[1].relay()
    for n, pos in ((0, py), (1, px)):
        s2[n].finish()
        c3[n, 0:2] = a1[n, 0:2, pos] + r2[n, 2] + r2[n, 4]
        c3[n, 2:4] = a1[n, 2:4, pos] + r2[n, 1] + r2[n, 5]
    s3 = Stage(lambda d, h: c3.at[h, d], r3, rs3_s, rs3_r, 2, pz)
    s3.begin()
    s3.relay()
    s3.finish()
    out_ref[:, 0:128] = c3[0, pz] + r3[2] + r3[4]
    out_ref[:, 128:256] = c3[1, pz] + r3[1] + r3[5]

    def q_drain(i, carry):
        q_copy(i).wait_send()
        return carry

    lax.fori_loop(tm + 1, TM, q_drain, 0)
    for i in range(1, NF):
        enc_copy(i).wait_send()
        s_copy(i).wait_send()

    @pl.when(tm < TM - 1)
    def _():
        id_copy.wait_send()

    for t in range(TILES):
        @pl.when(fq != OWNER[t])
        def _(t=t):
            n_copy(t).wait_send()

        @pl.when(fq == OWNER[t])
        def _(t=t):
            for i in range(1, NF):
                p_copy(t, i).wait_send()

    @pl.when((fq == NF - 1) & (tm < TM - 1))
    def _():
        for q in range(NF):
            halo_copy(q).wait_send()

    for stage in (sx, sy, s2[0], s2[1], s3):
        stage.drain()


def on_device(
    spectrum, decay_rate, init_state, clip_ids, encoder, gauss_noise, uniform_noise, boost_count, templates,
):
    vmem = pl.BlockSpec(memory_space=pltpu.VMEM)
    hbm = pl.BlockSpec(memory_space=pl.ANY)
    V = pltpu.VMEM
    dma = pltpu.SemaphoreType.DMA
    loss, grad = pl.pallas_call(
        kernel,
        out_shape=(
            jax.ShapeDtypeStruct((1, FRAMES), f32),
            jax.ShapeDtypeStruct((K * L // TM, BINS), f32),
        ),
        in_specs=[vmem] * 6 + [hbm] * 3,
        out_specs=(vmem, vmem),
        scratch_shapes=[
            V((BINS, K * L), bf16), V((2, K, 128), f32), V((2, 2, K, 128), f32), V((NF, K, BINS), bf16),
            V((BINS, FRAMES), f32), V((BINS, FRAMES), f32), V((TILES, BINS, 128), bf16),
            V((2, NF, BINS, 128), bf16), V((TILES + 1, K, 128), bf16), V((TILES + 1, K, 128), f32),
            V((1, 128), jnp.int32), V((1, BINS), f32), V((TM, 1, BINS), f32), V((K * L, FRAMES), bf16),
            V((BINS, FRAMES), f32), V((NF, 8, FRAMES), f32), V((BINS, FRAMES), bf16),
            V((2, 4, 4, 4, 64, 128), f32), V((2, 4, 4, 64, 128), f32), V((2, 4, 64, 128), f32),
            V((2, 6, 2, 4, 64, 128), f32), V((2, 6, 2, 64, 128), f32), V((6, 64, 128), f32),
            dma((5,)), dma((NF,)), dma((NF,)), dma((TM,)), dma((TM,)), dma, dma,
            dma((TILES,)), dma((2, NF)), dma((TILES, NF)), dma((TILES,)), dma((NF,)), dma,
            dma((NF,)), dma((NF,)),
            dma((2, 6)), dma((2, 6)), dma((2, 6)), dma((2, 6)), dma((6,)), dma((6,)),
        ],
        compiler_params=pltpu.CompilerParams(
            collective_id=0, has_side_effects=True, vmem_limit_bytes=56 * 1024 * 1024),
        name="topic_step",
    )(
        spectrum, decay_rate.reshape(1, BINS), init_state.reshape(1, BINS), clip_ids.reshape(1, FRAMES),
        encoder, boost_count.reshape(1, K), gauss_noise, uniform_noise, templates,
    )
    return loss.reshape(FRAMES), grad


def solution(mesh):
    placed = (
        P("freq", "tm"), P("freq"), P("freq"), P("tm"), P(None, "freq"), P(None, "tm"),
        P(None, None, "tm"), P(), P("freq", None),
    )
    return jax.shard_map(
        on_device, mesh=mesh, in_specs=placed, out_specs=(P("tm"), P("tm", "freq")), check_vma=False
    )
```

time: 2010 us -> 91 us (0.05)
  waiting for transfers between devices: 1190 us -> 0 us
  blocking collectives: 576 us -> 0 us
  local copies, waits for them, and re-layouts: 124 us -> 2.74 us
  Pallas kernels: 0 us -> 86.2 us
  other arithmetic: 69.7 us -> 1.28 us
    psum x2 -> x0, waiting for transfers between devices: 1190 us -> none  [the longest x1 752 us: on_device(): total_grad = lax.psum(full_grad, 'tm')]
    all_gather x2 -> x0, blocking collectives: 378 us -> none  [prefix(): gathered = jax.tree.map(lambda a: lax.all_gather(a, axis), part)]
    unnamed x1 -> x0, blocking collectives: 188 us -> none
    pallas_call x0 -> x1, Pallas kernels: none -> 86.2 us  [on_device(): pl.pallas_call(kernel, out_shape=(jax.ShapeDtypeStruct((1, FRAMES), f32),...]
    slice x70 -> x0, local copies, waits for them, and re-layouts: 82.2 us -> none  [the longest x66 77.9 us: on_device(): running, summed = lax.associative_scan(compose, (rates, inputs), axis=1)]
    mul x21 -> x0, other arithmetic: 31.6 us -> none  [the longest x17 21.9 us: compose(): return (former[0] * latter[0], latter[0] * former[1] + latter[1])]
  transfers between devices with their start and end apart: 3 -> 0, of which waited for: 3 -> 0; matrix products, arithmetic and copies ran while one was open for 0% -> 0% of each run, Pallas kernels for 0% -> 0%
where the time goes in v1:
time: 91 us; the launch traced here: 90.8 us
  Pallas kernels  86.2 us (95%)
  local copies, waits for them, and re-layouts  2.74 us (3%)
  other arithmetic  1.28 us (1%)
    pallas_call x1, Pallas kernels, on_device(): pl.pallas_call(kernel, out_shape=(jax.ShapeDtypeStruct((1, FRAMES), f32),...  86.2 us

profile of v1, /device:TPU:32, one launch (start us, length us, event | category | flops | bytes accessed | tf_op | source)
XLA Modules:
  0.0 90.8 jit_solution(2437944163419348839)
XLA Ops:
  0.6 1.3 %reshape.21.ids_ref = s32[1,768]{1,0:T(1,128)} reshape(s32[768]{0:T(1024)} %param.12) | data formatting | bytes 6144 | tf_op jit(solution)/shard_map/reshape | solution.py:454
  1.9 86.2 %topic_step.1 = (f32[1,768]{1,0:T(1,128)}, f32[64,256]{1,0:T(8,128)}) custom-call(bf16[256,768]{1,0:T(8,128)(2,1)} %spec_ref.1, f32[1,256]{1,0:T(1,128)} %bitcast.3, f32[1,256]{1,0:T(1,128)} %bitcast.4, s32[1,768]{1,0:T(1,128)} %reshape.21.ids_ref, bf16[256,256]{1,0:T(8,128)(2,1)} %enc_ref.1, s32[1,256]{1,0:T(1,128)} %bitcast.5, f32[256,768]{1,0:T(8,128)} %gauss_hbm.1, ...), custom_call_target="tpu_custom_call" | custom-call | tf_op jit(solution)/shard_map/topic_step/pallas_call | solution.py:429
  88.1 1.3 %reduce = f32[768]{0:T(1024)} reduce(f32[1,768]{1,0:T(1,128)} %get-tuple-element.4, f32[]{:T(128)} %constant), dimensions={0}, to_apply=%get-tuple-element.4.reduce_sub_computation | reduce | bytes 6148 | tf_op jit(solution)/shard_map/topic_step/pallas_call | solution.py:429
  89.3 1.5 %copy.12 = f32[64,256]{1,0:T(8,128)} copy(f32[64,256]{1,0:T(8,128)} %get-tuple-element.9) | data formatting | bytes 131072

commit v2 on v1

--- a/solution.py
+++ b/solution.py
@@ -20,6 +20,7 @@
 LOG_GAIN = 0.22314355131420976
 OWNER = (0, 0, 1, 2, 2, 3)
 SLOT = (0, 1, 0, 0, 1, 0)
+ORDER = (2, 1, 3, 0)
 
 
 def remote(src, dst, send, recv, tm, fq):
@@ -32,8 +33,8 @@
 def kernel(
     spec_ref, decay_ref, init_ref, ids_ref, enc_ref, boost_ref, gauss_hbm, unif_hbm, tmpl_hbm,
     loss_ref, out_ref,
-    tmpl, gbuf, ubuf, encf, grow, cum, normed, nbuf, pbuf, pf, idh, qsend, qbuf, st,
-    recon, sbuf, rat, grad, a1, c3, r1, r2, r3,
+    tmpl, gbuf, ubuf, encf, grow, cum, normed, nbuf, pbuf, pf, idh, qbuf, st,
+    recon, sbuf, rat, grad, w1, a1, c3, r1, r2, r3,
     load_sem, enc_s, enc_r, q_s, q_r, id_s, id_r, n_s, n_r, p_s, p_r, h_s, h_r, s_s, s_r,
     rs1_s, rs1_r, rs2_s, rs2_r, rs3_s, rs3_r,
 ):
@@ -45,17 +46,23 @@
     nxt = lax.rem(tm + 1, TM)
     prv = lax.rem(tm + TM - 1, TM)
 
-    def greet(i, carry):
+    px = lax.rem(tm, 4)
+    py = lax.rem(tm // 4, 4)
+    pz = tm // 16
+
+    def along(axis, step):
+        if axis == 0:
+            return tm - px + lax.rem(px + step, 4)
+        if axis == 1:
+            return tm - 4 * py + 4 * lax.rem(py + step, 4)
+        return tm - 16 * pz + 16 * lax.rem(pz + step, 4)
+
+    peers = [(along(axis, step), fq) for axis in range(3) for step in range(1, 4)]
+    peers += [(tm, lax.rem(fq + i, NF)) for i in range(1, NF)]
+    peers += [(place, lax.rem(fq + i, NF)) for place in (nxt, prv) for i in range(NF)]
+    for place, other in peers:
         pl.semaphore_signal(
-            barrier, inc=1, device_id={"tm": lax.rem(tm + i, TM), "freq": fq}, device_id_type=MESH)
-        return carry
-
-    lax.fori_loop(1, TM, greet, 0)
-    for i in range(1, NF):
-        other = lax.rem(fq + i, NF)
-        for place in (tm, nxt, prv):
-            pl.semaphore_signal(
-                barrier, inc=1, device_id={"tm": place, "freq": other}, device_id_type=MESH)
+            barrier, inc=1, device_id={"tm": place, "freq": other}, device_id_type=MESH)
 
     first = zlo * 3 + core * 2
     load_t = pltpu.make_async_copy(tmpl_hbm, tmpl, load_sem.at[0])
@@ -113,18 +120,33 @@
         cum[:, span] = c
         carry = c[:, 255:256]
     q_col = carry * jnp.exp(log_col * float(FRAMES))
-    qsend[...] = row_of(q_col)
-
-    pl.semaphore_wait(barrier, TM - 1 + 3 * (NF - 1))
-
-    def q_copy(place):
-        return remote(qsend, qbuf.at[tm], q_s.at[place], q_r.at[tm], place, fq)
-
-    def q_start(i, carry):
-        q_copy(i).start()
-        return carry
-
-    lax.fori_loop(tm + 1, TM, q_start, 0)
+    positions = (px, py, pz)
+
+    def q_copy(axis, step):
+        pos = positions[axis]
+        return remote(
+            qbuf.at[axis, pos], qbuf.at[axis, pos], q_s.at[axis, step], q_r.at[axis, step], along(axis, step), fq)
+
+    def q_send(axis, row):
+        qbuf[axis, positions[axis]] = row
+        for step in range(1, 4):
+            q_copy(axis, step).start()
+
+    def q_take(axis, jump):
+        pos = positions[axis]
+        for step in range(1, 4):
+            slot = qbuf.at[axis, lax.rem(pos + 4 - step, 4)]
+            remote(slot, slot, q_s.at[axis, step], q_r.at[axis, step], tm, fq).wait_recv()
+        ahead = jnp.zeros((1, BINS), f32)
+        total = jnp.zeros((1, BINS), f32)
+        for j in range(4):
+            ahead = jnp.where(j < pos, jump * ahead + qbuf[axis, j], ahead)
+            total = jump * total + qbuf[axis, j]
+        return ahead, total
+
+    q_row = row_of(q_col)
+    pl.semaphore_wait(barrier, len(peers))
+    q_send(0, q_row)
 
     def enc_copy(i):
         return remote(enc_ref, encf.at[fq], enc_s.at[i], enc_r.at[i], tm, lax.rem(fq + i, NF))
@@ -152,13 +174,16 @@
     def _():
         ready_noise(1)
 
-    def q_wait(j, carry):
-        remote(qsend, qbuf.at[j], q_s.at[j], q_r.at[j], tm, fq).wait_recv()
-        return carry
-
-    lax.fori_loop(0, tm, q_wait, 0)
-    jump = jnp.exp(log_row * float(FRAMES))
-    entry = lax.fori_loop(0, tm, lambda j, e: jump * e + qbuf[j], init_ref[...])
+    entry = jnp.zeros((1, BINS), f32)
+    gain = jnp.ones((1, BINS), f32)
+    for axis in range(3):
+        frames = float(FRAMES * 4 ** axis)
+        ahead, total = q_take(axis, jnp.exp(log_row * frames))
+        if axis < 2:
+            q_send(axis + 1, total)
+        entry += gain * ahead
+        gain = gain * jnp.exp(log_row * (frames * positions[axis].astype(f32)))
+    entry += gain * init_ref[...]
     entry_col = column(entry)
     for t in range(TILES):
         span = slice(t * 128, t * 128 + 128)
@@ -298,100 +323,140 @@
     part = scale / spec_sum
     rat[...] = (plain - part * recon[...]).astype(bf16)
 
-    def grads(z, carry):
+    def gradient(n):
+        z = lax.rem(pz + ORDER[n], 4)
         g = lax.dot_general(
             st[pl.ds(pl.multiple_of(z * 1024, 1024), 1024), :], rat[...],
-            (((1,), (1,)), ((), ())), preferred_element_type=f32)
-        g = g.reshape(4, 4, 64, 256)
-        grad[0, z] = g[..., 0:128]
-        grad[1, z] = g[..., 128:256]
-        return carry
-
-    lax.fori_loop(0, 4, grads, 0)
-
-    px = lax.rem(tm, 4)
-    py = lax.rem(tm // 4, 4)
-    pz = tm // 16
-
-    def along(axis, step):
-        if axis == 0:
-            return tm - px + lax.rem(px + step, 4)
-        if axis == 1:
-            return tm - 4 * py + 4 * lax.rem(py + step, 4)
-        return tm - 16 * pz + 16 * lax.rem(pz + step, 4)
-
-    class Stage:
-        def __init__(self, view, buf, send, recv, axis, pos):
-            self.view, self.buf, self.send, self.recv = view, buf, send, recv
-            self.right, self.left = along(axis, 1), along(axis, 3)
-            self.p1, self.p2, self.p3 = (lax.rem(pos + i, 4) for i in (1, 2, 3))
+            (((1,), (1,)), ((), ())), preferred_element_type=f32).reshape(4, 4, 64, 256)
+        grad[n, 0] = g[..., 0:128]
+        grad[n, 1] = g[..., 128:256]
+
+    class Ring:
+        def __init__(self, view, buf, send, recv, axis, staged=None):
+            self.view, self.buf, self.send, self.recv, self.staged = view, buf, send, recv, staged
+            self.pos = positions[axis]
+            to = (along(axis, 1), along(axis, 3))
+            far, right, left = (lax.rem(self.pos + i, 4) for i in (2, 1, 3))
+            self.parts = (
+                (far, 0, to[0]), (right, 1, to[0]), (right, 0, to[0]),
+                (far, 1, to[1]), (left, 0, to[1]), (left, 1, to[1]),
+            )
 
         def copy(self, n):
-            d, h, to = (
-                (self.p2, 0, self.right), (self.p1, 1, self.right), (self.p1, 0, self.right),
-                (self.p2, 1, self.left), (self.p3, 0, self.left), (self.p3, 1, self.left),
-            )[n]
-            return remote(
-                self.view(d, h), self.buf.at[n], self.send.at[n], self.recv.at[n], to, fq)
+            d, h, to = self.parts[n]
+            src = self.view(d, h) if self.staged is None else self.staged.at[n]
+            return remote(src, self.buf.at[n], self.send.at[n], self.recv.at[n], to, fq)
+
+        def push(self, n, more=None):
+            view = self.view(self.parts[n][0], self.parts[n][1])
+            if self.staged is not None:
+                value = view[...]
+                if more is not None:
+                    value = value + self.buf[more].astype(f32)
+                self.staged[n] = value.astype(self.staged.dtype)
+            elif more is not None:
+                view[...] = view[...] + self.buf[more]
+            self.copy(n).start()
 
         def begin(self):
             for n in (0, 3, 1, 4):
-                self.copy(n).start()
+                self.push(n)
 
         def relay(self):
-            self.copy(0).wait_recv()
-            v = self.view(self.p1, 0)
-            v[...] = v[...] + self.buf[0]
-            self.copy(2).start()
-            self.copy(3).wait_recv()
-            v = self.view(self.p3, 1)
-            v[...] = v[...] + self.buf[3]
-            self.copy(5).start()
-
-        def finish(self):
+            for n in (0, 3):
+                self.copy(n).wait_recv()
+                self.push(n + 2, n)
+
+        def result(self):
             for n in (1, 4, 2, 5):
                 self.copy(n).wait_recv()
+            return tuple(
+                self.view(self.pos, h)[...] + self.buf[l].astype(f32) + self.buf[r].astype(f32)
+                for h, l, r in ((0, 2, 4), (1, 1, 5)))
 
         def drain(self):
             for n in range(6):
                 self.copy(n).wait_send()
 
-    sx = Stage(lambda d, h: grad.at[0, pl.ds(2 * h, 2), :, d], r1.at[0], rs1_s.at[0], rs1_r.at[0], 0, px)
-    sy = Stage(lambda d, h: grad.at[1, pl.ds(2 * h, 2), d, :], r1.at[1], rs1_s.at[1], rs1_r.at[1], 1, py)
-    sx.begin()
-    sy.begin()
-    sx.relay()
-    sy.relay()
-    sx.finish()
-    a1[0, 0:2] = grad[0, 0:2, :, px] + r1[0, 2] + r1[0, 4]
-    a1[0, 2:4] = grad[0, 2:4, :, px] + r1[0, 1] + r1[0, 5]
-    s2 = [
-        Stage(lambda d, h: a1.at[0, pl.ds(2 * h, 2), d], r2.at[0], rs2_s.at[0], rs2_r.at[0], 1, py),
-        Stage(lambda d, h: a1.at[1, pl.ds(2 * h, 2), d], r2.at[1], rs2_s.at[1], rs2_r.at[1], 0, px),
-    ]
-    s2[0].begin()
-    sy.finish()
-    a1[1, 0:2] = grad[1, 0:2, py] + r1[1, 2] + r1[1, 4]
-    a1[1, 2:4] = grad[1, 2:4, py] + r1[1, 1] + r1[1, 5]
-    s2[1].begin()
-    s2[0].relay()
-    s2[1].relay()
-    for n, pos in ((0, py), (1, px)):
-        s2[n].finish()
-        c3[n, 0:2] = a1[n, 0:2, pos] + r2[n, 2] + r2[n, 4]
-        c3[n, 2:4] = a1[n, 2:4, pos] + r2[n, 1] + r2[n, 5]
-    s3 = Stage(lambda d, h: c3.at[h, d], r3, rs3_s, rs3_r, 2, pz)
-    s3.begin()
-    s3.relay()
-    s3.finish()
-    out_ref[:, 0:128] = c3[0, pz] + r3[2] + r3[4]
-    out_ref[:, 128:256] = c3[1, pz] + r3[1] + r3[5]
-
-    def q_drain(i, carry):
-        q_copy(i).wait_send()
-        return carry
-
-    lax.fori_loop(tm + 1, TM, q_drain, 0)
+    s1 = [[
+        Ring(lambda d, h, n=n: grad.at[n, 0, pl.ds(2 * h, 2), d], r1.at[n, 0], rs1_s.at[n, 0], rs1_r.at[n, 0], 0, w1.at[n, 0]),
+        Ring(lambda d, h, n=n: grad.at[n, 1, d, pl.ds(2 * h, 2)], r1.at[n, 1], rs1_s.at[n, 1], rs1_r.at[n, 1], 1, w1.at[n, 1]),
+    ] for n in range(4)]
+    s2 = [[
+        Ring(lambda d, h, n=n, c=c: a1.at[n, c, d, pl.ds(32 * h, 32)], r2.at[n, c], rs2_s.at[n, c], rs2_r.at[n, c], 1 - c)
+        for c in range(2)] for n in range(4)]
+    z_to = (along(2, 1), along(2, 3))
+
+    def z_copy(n):
+        piece, half = ((0, 0), (1, 1), (1, 0), (0, 1), (2, 0), (2, 1))[n]
+        return remote(c3.at[piece, half], r3.at[n], rs3_s.at[n], rs3_r.at[n], z_to[n // 3], fq)
+
+    def begin1(n):
+        for ring in s1[n]:
+            ring.begin()
+
+    def relay1(n):
+        for ring in s1[n]:
+            ring.relay()
+
+    def begin2(n):
+        for c in range(2):
+            top, low = s1[n][c].result()
+            a1[n, c, 0:2] = top
+            a1[n, c, 2:4] = low
+            s2[n][c].begin()
+
+    def relay2(n):
+        for ring in s2[n]:
+            ring.relay()
+
+    def done2(n):
+        for c in range(2):
+            top, low = s2[n][c].result()
+            c3[n, c, 0:32] = top
+            c3[n, c, 32:64] = low
+        if n == 0:
+            z_copy(0).start()
+            z_copy(3).start()
+        elif n < 3:
+            half, plain, held = ((1, 1, 0), (0, 4, 3))[n - 1]
+            z_copy(plain).start()
+            z_copy(held).wait_recv()
+            c3[n, 1 - half] = c3[n, 1 - half] + r3[held]
+            z_copy((2, 5)[n - 1]).start()
+
+    gradient(0)
+    begin1(0)
+    gradient(1)
+    begin1(1)
+    gradient(2)
+    relay1(0)
+    begin1(2)
+    gradient(3)
+    relay1(1)
+    begin1(3)
+    begin2(0)
+    relay1(2)
+    begin2(1)
+    relay2(0)
+    relay1(3)
+    begin2(2)
+    relay2(1)
+    done2(0)
+    begin2(3)
+    relay2(2)
+    done2(1)
+    relay2(3)
+    done2(2)
+    done2(3)
+    for n in (1, 4, 2, 5):
+        z_copy(n).wait_recv()
+    out_ref[:, 0:128] = c3[3, 0] + r3[2] + r3[4]
+    out_ref[:, 128:256] = c3[3, 1] + r3[1] + r3[5]
+
+    for axis in range(3):
+        for step in range(1, 4):
+            q_copy(axis, step).wait_send()
     for i in range(1, NF):
         enc_copy(i).wait_send()
         s_copy(i).wait_send()
@@ -415,8 +480,11 @@
         for q in range(NF):
             halo_copy(q).wait_send()
 
-    for stage in (sx, sy, s2[0], s2[1], s3):
-        stage.drain()
+    for n in range(4):
+        for ring in s1[n] + s2[n]:
+            ring.drain()
+    for n in range(6):
+        z_copy(n).wait_send()
 
 
 def on_device(
@@ -438,14 +506,14 @@
             V((BINS, K * L), bf16), V((2, K, 128), f32), V((2, 2, K, 128), f32), V((NF, K, BINS), bf16),
             V((BINS, FRAMES), f32), V((BINS, FRAMES), f32), V((TILES, BINS, 128), bf16),
             V((2, NF, BINS, 128), bf16), V((TILES + 1, K, 128), bf16), V((TILES + 1, K, 128), f32),
-            V((1, 128), jnp.int32), V((1, BINS), f32), V((TM, 1, BINS), f32), V((K * L, FRAMES), bf16),
+            V((1, 128), jnp.int32), V((3, 4, 1, BINS), f32), V((K * L, FRAMES), bf16),
             V((BINS, FRAMES), f32), V((NF, 8, FRAMES), f32), V((BINS, FRAMES), bf16),
-            V((2, 4, 4, 4, 64, 128), f32), V((2, 4, 4, 64, 128), f32), V((2, 4, 64, 128), f32),
-            V((2, 6, 2, 4, 64, 128), f32), V((2, 6, 2, 64, 128), f32), V((6, 64, 128), f32),
-            dma((5,)), dma((NF,)), dma((NF,)), dma((TM,)), dma((TM,)), dma, dma,
+            V((4, 2, 4, 4, 64, 128), f32), V((4, 2, 6, 2, 64, 128), bf16), V((4, 2, 4, 64, 128), f32),
+            V((4, 2, 64, 128), f32), V((4, 2, 6, 2, 64, 128), bf16), V((4, 2, 6, 32, 128), f32), V((6, 64, 128), f32),
+            dma((5,)), dma((NF,)), dma((NF,)), dma((3, 4)), dma((3, 4)), dma, dma,
             dma((TILES,)), dma((2, NF)), dma((TILES, NF)), dma((TILES,)), dma((NF,)), dma,
             dma((NF,)), dma((NF,)),
-            dma((2, 6)), dma((2, 6)), dma((2, 6)), dma((2, 6)), dma((6,)), dma((6,)),
+            dma((4, 2, 6)), dma((4, 2, 6)), dma((4, 2, 6)), dma((4, 2, 6)), dma((6,)), dma((6,)),
         ],
         compiler_params=pltpu.CompilerParams(
             collective_id=0, has_side_effects=True, vmem_limit_bytes=56 * 1024 * 1024),

time: 91 us -> 78.7 us (0.86)
  Pallas kernels: 86.2 us -> 73.8 us
    pallas_call x1, Pallas kernels: 86.2 us -> 73.8 us  [on_device(): pl.pallas_call(kernel, out_shape=(jax.ShapeDtypeStruct((1, FRAMES), f32),...]
where the time goes in v2:
time: 78.7 us; the launch traced here: 78.4 us
  Pallas kernels  73.8 us (94%)
  local copies, waits for them, and re-layouts  2.74 us (3%)
  other arithmetic  1.28 us (2%)
    pallas_call x1, Pallas kernels, on_device(): pl.pallas_call(kernel, out_shape=(jax.ShapeDtypeStruct((1, FRAMES), f32),...  73.8 us

profile of v2, /device:TPU:32, one launch (start us, length us, event | category | flops | bytes accessed | tf_op | source)
XLA Modules:
  0.0 78.4 jit_solution(15106077385926132800)
XLA Ops:
  0.6 1.3 %reshape.21.ids_ref = s32[1,768]{1,0:T(1,128)} reshape(s32[768]{0:T(1024)} %param.12) | data formatting | bytes 6144 | tf_op jit(solution)/shard_map/reshape | solution.py:522
  1.9 73.8 %topic_step.1 = (f32[1,768]{1,0:T(1,128)}, f32[64,256]{1,0:T(8,128)}) custom-call(bf16[256,768]{1,0:T(8,128)(2,1)} %spec_ref.1, f32[1,256]{1,0:T(1,128)} %bitcast.3, f32[1,256]{1,0:T(1,128)} %bitcast.4, s32[1,768]{1,0:T(1,128)} %reshape.21.ids_ref, bf16[256,256]{1,0:T(8,128)(2,1)} %enc_ref.1, s32[1,256]{1,0:T(1,128)} %bitcast.5, f32[256,768]{1,0:T(8,128)} %gauss_hbm.1, ...), custom_call_target="tpu_custom_call" | custom-call | tf_op jit(solution)/shard_map/topic_step/pallas_call | solution.py:497
  75.7 1.3 %reduce = f32[768]{0:T(1024)} reduce(f32[1,768]{1,0:T(1,128)} %get-tuple-element.4, f32[]{:T(128)} %constant), dimensions={0}, to_apply=%get-tuple-element.4.reduce_sub_computation | reduce | bytes 6148 | tf_op jit(solution)/shard_map/topic_step/pallas_call | solution.py:497
  77.0 1.5 %copy.12 = f32[64,256]{1,0:T(8,128)} copy(f32[64,256]{1,0:T(8,128)} %get-tuple-element.9) | data formatting | bytes 131072

commit v3 on v2

--- a/solution.py
+++ b/solution.py
@@ -34,7 +34,7 @@
     spec_ref, decay_ref, init_ref, ids_ref, enc_ref, boost_ref, gauss_hbm, unif_hbm, tmpl_hbm,
     loss_ref, out_ref,
     tmpl, gbuf, ubuf, encf, grow, cum, normed, nbuf, pbuf, pf, idh, qbuf, st,
-    recon, sbuf, rat, grad, w1, a1, c3, r1, r2, r3,
+    recon, sbuf, rat, grad, w1, a1, c3, r1, r1f, r2, r3,
     load_sem, enc_s, enc_r, q_s, q_r, id_s, id_r, n_s, n_r, p_s, p_r, h_s, h_r, s_s, s_r,
     rs1_s, rs1_r, rs2_s, rs2_r, rs3_s, rs3_r,
 ):
@@ -44,7 +44,6 @@
     zlo = fq // 2
     barrier = pltpu.get_barrier_semaphore()
     nxt = lax.rem(tm + 1, TM)
-    prv = lax.rem(tm + TM - 1, TM)
 
     px = lax.rem(tm, 4)
     py = lax.rem(tm // 4, 4)
@@ -59,7 +58,6 @@
 
     peers = [(along(axis, step), fq) for axis in range(3) for step in range(1, 4)]
     peers += [(tm, lax.rem(fq + i, NF)) for i in range(1, NF)]
-    peers += [(place, lax.rem(fq + i, NF)) for place in (nxt, prv) for i in range(NF)]
     for place, other in peers:
         pl.semaphore_signal(
             barrier, inc=1, device_id={"tm": place, "freq": other}, device_id_type=MESH)
@@ -153,12 +151,6 @@
 
     for i in range(1, NF):
         enc_copy(i).start()
-    id_copy = remote(ids_ref.at[:, pl.ds(FRAMES - 128, 128)], idh, id_s, id_r, nxt, fq)
-
-    @pl.when(tm < TM - 1)
-    def _():
-        id_copy.start()
-
     encf[fq] = enc_ref[...]
 
     boost = column(boost_ref[...].astype(f32))
@@ -184,6 +176,12 @@
         entry += gain * ahead
         gain = gain * jnp.exp(log_row * (frames * positions[axis].astype(f32)))
     entry += gain * init_ref[...]
+    id_copy = remote(ids_ref.at[:, pl.ds(FRAMES - 128, 128)], idh, id_s, id_r, nxt, fq)
+
+    @pl.when(tm < TM - 1)
+    def _():
+        id_copy.start()
+
     entry_col = column(entry)
     for t in range(TILES):
         span = slice(t * 128, t * 128 + 128)
@@ -344,18 +342,15 @@
 
         def copy(self, n):
             d, h, to = self.parts[n]
-            src = self.view(d, h) if self.staged is None else self.staged.at[n]
-            return remote(src, self.buf.at[n], self.send.at[n], self.recv.at[n], to, fq)
+            src = self.view(d, h) if self.staged is None or n % 3 == 2 else self.staged.at[n]
+            return remote(src, self.buf(n), self.send.at[n], self.recv.at[n], to, fq)
 
         def push(self, n, more=None):
             view = self.view(self.parts[n][0], self.parts[n][1])
-            if self.staged is not None:
-                value = view[...]
-                if more is not None:
-                    value = value + self.buf[more].astype(f32)
-                self.staged[n] = value.astype(self.staged.dtype)
-            elif more is not None:
-                view[...] = view[...] + self.buf[more]
+            if more is not None:
+                view[...] = view[...] + self.buf(more)[...].astype(f32)
+            elif self.staged is not None:
+                self.staged[n] = view[...].astype(self.staged.dtype)
             self.copy(n).start()
 
         def begin(self):
@@ -371,19 +366,22 @@
             for n in (1, 4, 2, 5):
                 self.copy(n).wait_recv()
             return tuple(
-                self.view(self.pos, h)[...] + self.buf[l].astype(f32) + self.buf[r].astype(f32)
+                self.view(self.pos, h)[...] + self.buf(l)[...].astype(f32) + self.buf(r)[...].astype(f32)
                 for h, l, r in ((0, 2, 4), (1, 1, 5)))
 
         def drain(self):
             for n in range(6):
                 self.copy(n).wait_send()
 
+    def landing(n, c):
+        return lambda i: r1f.at[n, c, i // 3] if i % 3 == 2 else r1.at[n, c, i]
+
     s1 = [[
-        Ring(lambda d, h, n=n: grad.at[n, 0, pl.ds(2 * h, 2), d], r1.at[n, 0], rs1_s.at[n, 0], rs1_r.at[n, 0], 0, w1.at[n, 0]),
-        Ring(lambda d, h, n=n: grad.at[n, 1, d, pl.ds(2 * h, 2)], r1.at[n, 1], rs1_s.at[n, 1], rs1_r.at[n, 1], 1, w1.at[n, 1]),
+        Ring(lambda d, h, n=n: grad.at[n, 0, pl.ds(2 * h, 2), d], landing(n, 0), rs1_s.at[n, 0], rs1_r.at[n, 0], 0, w1.at[n, 0]),
+        Ring(lambda d, h, n=n: grad.at[n, 1, d, pl.ds(2 * h, 2)], landing(n, 1), rs1_s.at[n, 1], rs1_r.at[n, 1], 1, w1.at[n, 1]),
     ] for n in range(4)]
     s2 = [[
-        Ring(lambda d, h, n=n, c=c: a1.at[n, c, d, pl.ds(32 * h, 32)], r2.at[n, c], rs2_s.at[n, c], rs2_r.at[n, c], 1 - c)
+        Ring(lambda d, h, n=n, c=c: a1.at[n, c, d, pl.ds(32 * h, 32)], lambda i, n=n, c=c: r2.at[n, c, i], rs2_s.at[n, c], rs2_r.at[n, c], 1 - c)
         for c in range(2)] for n in range(4)]
     z_to = (along(2, 1), along(2, 3))
 
@@ -509,7 +507,7 @@
             V((1, 128), jnp.int32), V((3, 4, 1, BINS), f32), V((K * L, FRAMES), bf16),
             V((BINS, FRAMES), f32), V((NF, 8, FRAMES), f32), V((BINS, FRAMES), bf16),
             V((4, 2, 4, 4, 64, 128), f32), V((4, 2, 6, 2, 64, 128), bf16), V((4, 2, 4, 64, 128), f32),
-            V((4, 2, 64, 128), f32), V((4, 2, 6, 2, 64, 128), bf16), V((4, 2, 6, 32, 128), f32), V((6, 64, 128), f32),
+            V((4, 2, 64, 128), f32), V((4, 2, 6, 2, 64, 128), bf16), V((4, 2, 2, 2, 64, 128), f32), V((4, 2, 6, 32, 128), f32), V((6, 64, 128), f32),
             dma((5,)), dma((NF,)), dma((NF,)), dma((3, 4)), dma((3, 4)), dma, dma,
             dma((TILES,)), dma((2, NF)), dma((TILES, NF)), dma((TILES,)), dma((NF,)), dma,
             dma((NF,)), dma((NF,)),

time: 78.7 us -> 78.3 us (level)
  no operation moved by 1% of the time
where the time goes in v3:
time: 78.3 us; the launch traced here: 78.1 us
  Pallas kernels  73.4 us (94%)
  local copies, waits for them, and re-layouts  2.74 us (3%)
  other arithmetic  1.28 us (2%)
    pallas_call x1, Pallas kernels, on_device(): pl.pallas_call(kernel, out_shape=(jax.ShapeDtypeStruct((1, FRAMES), f32),...  73.4 us

profile of v3, /device:TPU:32, one launch (start us, length us, event | category | flops | bytes accessed | tf_op | source)
XLA Modules:
  0.0 78.1 jit_solution(6452577424443772519)
XLA Ops:
  0.6 1.3 %reshape.21.ids_ref = s32[1,768]{1,0:T(1,128)} reshape(s32[768]{0:T(1024)} %param.12) | data formatting | bytes 6144 | tf_op jit(solution)/shard_map/reshape | solution.py:520
  1.9 73.4 %topic_step.1 = (f32[1,768]{1,0:T(1,128)}, f32[64,256]{1,0:T(8,128)}) custom-call(bf16[256,768]{1,0:T(8,128)(2,1)} %spec_ref.1, f32[1,256]{1,0:T(1,128)} %bitcast.3, f32[1,256]{1,0:T(1,128)} %bitcast.4, s32[1,768]{1,0:T(1,128)} %reshape.21.ids_ref, bf16[256,256]{1,0:T(8,128)(2,1)} %enc_ref.1, s32[1,256]{1,0:T(1,128)} %bitcast.5, f32[256,768]{1,0:T(8,128)} %gauss_hbm.1, ...), custom_call_target="tpu_custom_call" | custom-call | tf_op jit(solution)/shard_map/topic_step/pallas_call | solution.py:495
  75.3 1.3 %reduce = f32[768]{0:T(1024)} reduce(f32[1,768]{1,0:T(1,128)} %get-tuple-element.4, f32[]{:T(128)} %constant), dimensions={0}, to_apply=%get-tuple-element.4.reduce_sub_computation | reduce | bytes 6148 | tf_op jit(solution)/shard_map/topic_step/pallas_call | solution.py:495
  76.6 1.5 %copy.12 = f32[64,256]{1,0:T(8,128)} copy(f32[64,256]{1,0:T(8,128)} %get-tuple-element.9) | data formatting | bytes 131072

commit v4 on v3

--- a/solution.py
+++ b/solution.py
@@ -30,10 +30,18 @@
     )
 
 
+def take(ref, sem):
+    remote(ref, ref, sem, sem, 0, 0).wait_recv()
+
+
+def sent(ref, sem):
+    remote(ref, ref, sem, sem, 0, 0).wait_send()
+
+
 def kernel(
-    spec_ref, decay_ref, init_ref, ids_ref, enc_ref, boost_ref, gauss_hbm, unif_hbm, tmpl_hbm,
+    decay_ref, init_ref, ids_ref, boost_ref, spec_hbm, enc_hbm, gauss_hbm, unif_hbm, tmpl_hbm,
     loss_ref, out_ref,
-    tmpl, gbuf, ubuf, encf, grow, cum, normed, nbuf, pbuf, pf, idh, qbuf, st,
+    spec_ref, tmpl, gbuf, ubuf, encf, grow, cum, normed, nbuf, pbuf, pf, idh, qbuf, st,
     recon, sbuf, rat, grad, w1, a1, c3, r1, r1f, r2, r3,
     load_sem, enc_s, enc_r, q_s, q_r, id_s, id_r, n_s, n_r, p_s, p_r, h_s, h_r, s_s, s_r,
     rs1_s, rs1_r, rs2_s, rs2_r, rs3_s, rs3_r,
@@ -62,9 +70,12 @@
         pl.semaphore_signal(
             barrier, inc=1, device_id={"tm": place, "freq": other}, device_id_type=MESH)
 
+    load_x = pltpu.make_async_copy(spec_hbm, spec_ref, load_sem.at[5])
+    load_x.start()
+    load_e = pltpu.make_async_copy(enc_hbm, encf.at[fq], load_sem.at[6])
+    load_e.start()
     first = zlo * 3 + core * 2
     load_t = pltpu.make_async_copy(tmpl_hbm, tmpl, load_sem.at[0])
-    load_t.start()
 
     def tile_loads(slot):
         cols = pl.ds(pl.multiple_of((first + slot) * 128, 128), 128)
@@ -80,6 +91,8 @@
     def _():
         for copy in tile_loads(1):
             copy.start()
+
+    load_t.start()
 
     rows = lax.broadcasted_iota(jnp.int32, (BINS, BINS), 0)
     cols = lax.broadcasted_iota(jnp.int32, (BINS, BINS), 1)
@@ -99,6 +112,7 @@
     decay_col = column(decay_row)
     ids = ids_ref[...].astype(f32)
     lift = jnp.exp(ids * LOG_GAIN)
+    load_x.wait()
     carry = jnp.zeros((BINS, 1), f32)
     for b in range(3):
         span = slice(b * 256, b * 256 + 256)
@@ -123,7 +137,7 @@
     def q_copy(axis, step):
         pos = positions[axis]
         return remote(
-            qbuf.at[axis, pos], qbuf.at[axis, pos], q_s.at[axis, step], q_r.at[axis, step], along(axis, step), fq)
+            qbuf.at[axis, pos], qbuf.at[axis, pos], q_s, q_r.at[axis], along(axis, step), fq)
 
     def q_send(axis, row):
         qbuf[axis, positions[axis]] = row
@@ -132,9 +146,7 @@
 
     def q_take(axis, jump):
         pos = positions[axis]
-        for step in range(1, 4):
-            slot = qbuf.at[axis, lax.rem(pos + 4 - step, 4)]
-            remote(slot, slot, q_s.at[axis, step], q_r.at[axis, step], tm, fq).wait_recv()
+        take(qbuf.at[axis, pl.ds(0, 3)], q_r.at[axis])
         ahead = jnp.zeros((1, BINS), f32)
         total = jnp.zeros((1, BINS), f32)
         for j in range(4):
@@ -147,12 +159,11 @@
     q_send(0, q_row)
 
     def enc_copy(i):
-        return remote(enc_ref, encf.at[fq], enc_s.at[i], enc_r.at[i], tm, lax.rem(fq + i, NF))
-
+        return remote(encf.at[fq], encf.at[fq], enc_s, enc_r, tm, lax.rem(fq + i, NF))
+
+    load_e.wait()
     for i in range(1, NF):
         enc_copy(i).start()
-    encf[fq] = enc_ref[...]
-
     boost = column(boost_ref[...].astype(f32))
 
     def ready_noise(slot):
@@ -191,7 +202,7 @@
 
     def n_copy(t):
         return remote(
-            normed.at[t], nbuf.at[SLOT[t], fq], n_s.at[t], n_r.at[SLOT[t], fq], tm, OWNER[t])
+            normed.at[t], nbuf.at[SLOT[t], fq], n_s, n_r.at[SLOT[t]], tm, OWNER[t])
 
     for t in (3, 4, 5, 0, 1, 2):
         @pl.when(fq != OWNER[t])
@@ -202,20 +213,16 @@
         def _(t=t):
             nbuf[SLOT[t], fq] = normed[t]
 
-    for i in range(1, NF):
-        src = lax.rem(fq + NF - i, NF)
-        remote(enc_ref, encf.at[src], enc_s.at[i], enc_r.at[i], tm, fq).wait_recv()
+    take(encf.at[pl.ds(0, 3)], enc_r)
 
     def p_copy(t, i):
-        return remote(pbuf.at[1 + t], pbuf.at[1 + t], p_s.at[t, i], p_r.at[t], tm, lax.rem(fq + i, NF))
+        return remote(pbuf.at[1 + t], pbuf.at[1 + t], p_s, p_r, tm, lax.rem(fq + i, NF))
 
     def halo_copy(q):
-        return remote(pbuf.at[TILES], pbuf.at[0], h_s.at[q], h_r, nxt, q)
+        return remote(pbuf.at[TILES], pbuf.at[0], h_s, h_r, nxt, q)
 
     def sample(slot):
-        for i in range(1, NF):
-            src = lax.rem(fq + i, NF)
-            remote(normed.at[0], nbuf.at[slot, src], n_s.at[0], n_r.at[slot, src], tm, fq).wait_recv()
+        take(nbuf.at[slot, pl.ds(0, 3)], n_r.at[slot])
         logits = jnp.dot(encf[0], nbuf[slot, 0], preferred_element_type=f32)
         for q in range(1, NF):
             logits += jnp.dot(encf[q], nbuf[slot, q], preferred_element_type=f32)
@@ -262,10 +269,13 @@
         id_copy.wait_recv()
         halo_copy(0).wait_recv()
 
-    for t in range(TILES):
-        @pl.when(fq != OWNER[t])
-        def _(t=t):
-            p_copy(t, 1).wait_recv()
+    @pl.when(core == 0)
+    def _():
+        take(pbuf.at[pl.ds(0, 4)], p_r)
+
+    @pl.when(core == 1)
+    def _():
+        take(pbuf.at[pl.ds(0, 5)], p_r)
 
     lane = lax.broadcasted_iota(jnp.int32, (L, 128), 1)
     lag = lax.broadcasted_iota(jnp.int32, (L, 128), 0)
@@ -293,7 +303,7 @@
             prior = current
         return carry
 
-    lax.fori_loop(0, K, build_row, 0, unroll=4)
+    lax.fori_loop(0, K, build_row, 0, unroll=16)
 
     load_t.wait()
     for b in range(3):
@@ -306,13 +316,11 @@
         sbuf[fq, 2:3, span] = jnp.sum(x * jnp.log(rec), axis=0, keepdims=True)
 
     def s_copy(i):
-        return remote(sbuf.at[fq], sbuf.at[fq], s_s.at[i], s_r.at[i], tm, lax.rem(fq + i, NF))
+        return remote(sbuf.at[fq], sbuf.at[fq], s_s, s_r, tm, lax.rem(fq + i, NF))
 
     for i in range(1, NF):
         s_copy(i).start()
-    for i in range(1, NF):
-        src = lax.rem(fq + NF - i, NF)
-        remote(sbuf.at[src], sbuf.at[src], s_s.at[i], s_r.at[i], tm, fq).wait_recv()
+    take(sbuf.at[pl.ds(0, 3)], s_r)
     sums = sbuf[0, 0:3, :] + sbuf[1, 0:3, :] + sbuf[2, 0:3, :] + sbuf[3, 0:3, :]
     recon_sum, spec_sum, log_sum = sums[0:1], sums[1:2], sums[2:3]
     loss_ref[...] = jnp.log(recon_sum) - log_sum / spec_sum
@@ -343,7 +351,7 @@
         def copy(self, n):
             d, h, to = self.parts[n]
             src = self.view(d, h) if self.staged is None or n % 3 == 2 else self.staged.at[n]
-            return remote(src, self.buf(n), self.send.at[n], self.recv.at[n], to, fq)
+            return remote(src, self.buf(n), self.send, self.recv.at[0 if n % 3 == 0 else 1], to, fq)
 
         def push(self, n, more=None):
             view = self.view(self.parts[n][0], self.parts[n][1])
@@ -359,45 +367,40 @@
 
         def relay(self):
             for n in (0, 3):
-                self.copy(n).wait_recv()
                 self.push(n + 2, n)
 
         def result(self):
-            for n in (1, 4, 2, 5):
-                self.copy(n).wait_recv()
             return tuple(
                 self.view(self.pos, h)[...] + self.buf(l)[...].astype(f32) + self.buf(r)[...].astype(f32)
                 for h, l, r in ((0, 2, 4), (1, 1, 5)))
 
-        def drain(self):
-            for n in range(6):
-                self.copy(n).wait_send()
-
     def landing(n, c):
         return lambda i: r1f.at[n, c, i // 3] if i % 3 == 2 else r1.at[n, c, i]
 
     s1 = [[
-        Ring(lambda d, h, n=n: grad.at[n, 0, pl.ds(2 * h, 2), d], landing(n, 0), rs1_s.at[n, 0], rs1_r.at[n, 0], 0, w1.at[n, 0]),
-        Ring(lambda d, h, n=n: grad.at[n, 1, d, pl.ds(2 * h, 2)], landing(n, 1), rs1_s.at[n, 1], rs1_r.at[n, 1], 1, w1.at[n, 1]),
+        Ring(lambda d, h, n=n: grad.at[n, 0, pl.ds(2 * h, 2), d], landing(n, 0), rs1_s, rs1_r.at[n], 0, w1.at[n, 0]),
+        Ring(lambda d, h, n=n: grad.at[n, 1, d, pl.ds(2 * h, 2)], landing(n, 1), rs1_s, rs1_r.at[n], 1, w1.at[n, 1]),
     ] for n in range(4)]
     s2 = [[
-        Ring(lambda d, h, n=n, c=c: a1.at[n, c, d, pl.ds(32 * h, 32)], lambda i, n=n, c=c: r2.at[n, c, i], rs2_s.at[n, c], rs2_r.at[n, c], 1 - c)
+        Ring(lambda d, h, n=n, c=c: a1.at[n, c, d, pl.ds(32 * h, 32)], lambda i, n=n, c=c: r2.at[n, c, i], rs2_s, rs2_r.at[n], 1 - c)
         for c in range(2)] for n in range(4)]
     z_to = (along(2, 1), along(2, 3))
 
     def z_copy(n):
         piece, half = ((0, 0), (1, 1), (1, 0), (0, 1), (2, 0), (2, 1))[n]
-        return remote(c3.at[piece, half], r3.at[n], rs3_s.at[n], rs3_r.at[n], z_to[n // 3], fq)
+        return remote(c3.at[piece, half], r3.at[n], rs3_s, rs3_r.at[(0, 2, 2, 1, 2, 2)[n]], z_to[n // 3], fq)
 
     def begin1(n):
         for ring in s1[n]:
             ring.begin()
 
     def relay1(n):
+        take(w1.at[n, 0, pl.ds(0, 4)], rs1_r.at[n, 0])
         for ring in s1[n]:
             ring.relay()
 
     def begin2(n):
+        take(w1.at[n], rs1_r.at[n, 1])
         for c in range(2):
             top, low = s1[n][c].result()
             a1[n, c, 0:2] = top
@@ -405,10 +408,12 @@
             s2[n][c].begin()
 
     def relay2(n):
+        take(r2.at[n, 0, pl.ds(0, 4)], rs2_r.at[n, 0])
         for ring in s2[n]:
             ring.relay()
 
     def done2(n):
+        take(r2.at[n, :, pl.ds(0, 4)], rs2_r.at[n, 1])
         for c in range(2):
             top, low = s2[n][c].result()
             c3[n, c, 0:32] = top
@@ -447,42 +452,35 @@
     relay2(3)
     done2(2)
     done2(3)
-    for n in (1, 4, 2, 5):
-        z_copy(n).wait_recv()
+    take(r3.at[pl.ds(0, 4)], rs3_r.at[2])
     out_ref[:, 0:128] = c3[3, 0] + r3[2] + r3[4]
     out_ref[:, 128:256] = c3[3, 1] + r3[1] + r3[5]
 
-    for axis in range(3):
-        for step in range(1, 4):
-            q_copy(axis, step).wait_send()
-    for i in range(1, NF):
-        enc_copy(i).wait_send()
-        s_copy(i).wait_send()
+    sent(qbuf.at[:, pl.ds(0, 3)], q_s)
+    sent(encf.at[pl.ds(0, 3)], enc_s)
+    sent(sbuf.at[pl.ds(0, 3)], s_s)
 
     @pl.when(tm < TM - 1)
     def _():
         id_copy.wait_send()
 
-    for t in range(TILES):
-        @pl.when(fq != OWNER[t])
-        def _(t=t):
-            n_copy(t).wait_send()
-
-        @pl.when(fq == OWNER[t])
-        def _(t=t):
-            for i in range(1, NF):
-                p_copy(t, i).wait_send()
+    @pl.when(core == 0)
+    def _():
+        sent(normed.at[pl.ds(0, 4)], n_s)
+        sent(pbuf.at[pl.ds(0, 6)], p_s)
+
+    @pl.when(core == 1)
+    def _():
+        sent(normed.at[pl.ds(0, 5)], n_s)
+        sent(pbuf.at[pl.ds(0, 3)], p_s)
 
     @pl.when((fq == NF - 1) & (tm < TM - 1))
     def _():
-        for q in range(NF):
-            halo_copy(q).wait_send()
-
-    for n in range(4):
-        for ring in s1[n] + s2[n]:
-            ring.drain()
-    for n in range(6):
-        z_copy(n).wait_send()
+        sent(pbuf.at[pl.ds(0, 4)], h_s)
+
+    sent(tmpl, rs1_s)
+    sent(recon, rs2_s)
+    sent(pbuf.at[pl.ds(0, 3)], rs3_s)
 
 
 def on_device(
@@ -498,27 +496,25 @@
             jax.ShapeDtypeStruct((1, FRAMES), f32),
             jax.ShapeDtypeStruct((K * L // TM, BINS), f32),
         ),
-        in_specs=[vmem] * 6 + [hbm] * 3,
+        in_specs=[vmem] * 4 + [hbm] * 5,
         out_specs=(vmem, vmem),
         scratch_shapes=[
-            V((BINS, K * L), bf16), V((2, K, 128), f32), V((2, 2, K, 128), f32), V((NF, K, BINS), bf16),
+            V((BINS, FRAMES), bf16), V((BINS, K * L), bf16), V((2, K, 128), f32), V((2, 2, K, 128), f32), V((NF, K, BINS), bf16),
             V((BINS, FRAMES), f32), V((BINS, FRAMES), f32), V((TILES, BINS, 128), bf16),
             V((2, NF, BINS, 128), bf16), V((TILES + 1, K, 128), bf16), V((TILES + 1, K, 128), f32),
             V((1, 128), jnp.int32), V((3, 4, 1, BINS), f32), V((K * L, FRAMES), bf16),
             V((BINS, FRAMES), f32), V((NF, 8, FRAMES), f32), V((BINS, FRAMES), bf16),
             V((4, 2, 4, 4, 64, 128), f32), V((4, 2, 6, 2, 64, 128), bf16), V((4, 2, 4, 64, 128), f32),
             V((4, 2, 64, 128), f32), V((4, 2, 6, 2, 64, 128), bf16), V((4, 2, 2, 2, 64, 128), f32), V((4, 2, 6, 32, 128), f32), V((6, 64, 128), f32),
-            dma((5,)), dma((NF,)), dma((NF,)), dma((3, 4)), dma((3, 4)), dma, dma,
-            dma((TILES,)), dma((2, NF)), dma((TILES, NF)), dma((TILES,)), dma((NF,)), dma,
-            dma((NF,)), dma((NF,)),
-            dma((4, 2, 6)), dma((4, 2, 6)), dma((4, 2, 6)), dma((4, 2, 6)), dma((6,)), dma((6,)),
+            dma((7,)), dma, dma, dma, dma((3,)), dma, dma, dma, dma((2,)), dma, dma, dma, dma, dma, dma,
+            dma, dma((4, 2)), dma, dma((4, 2)), dma, dma((3,)),
         ],
         compiler_params=pltpu.CompilerParams(
             collective_id=0, has_side_effects=True, vmem_limit_bytes=56 * 1024 * 1024),
         name="topic_step",
     )(
-        spectrum, decay_rate.reshape(1, BINS), init_state.reshape(1, BINS), clip_ids.reshape(1, FRAMES),
-        encoder, boost_count.reshape(1, K), gauss_noise, uniform_noise, templates,
+        decay_rate.reshape(1, BINS), init_state.reshape(1, BINS), clip_ids.reshape(1, FRAMES),
+        boost_count.reshape(1, K), spectrum, encoder, gauss_noise, uniform_noise, templates,
     )
     return loss.reshape(FRAMES), grad
 

time: 78.3 us -> 72.4 us (0.925)
  Pallas kernels: 73.4 us -> 67.1 us
    pallas_call x1, Pallas kernels: 73.4 us -> 67.1 us  [on_device(): pl.pallas_call(kernel, out_shape=(jax.ShapeDtypeStruct((1, FRAMES), f32),...]
where the time goes in v4:
time: 72.4 us; the launch traced here: 71.7 us
  Pallas kernels  67.1 us (93%)
  local copies, waits for them, and re-layouts  2.74 us (4%)
  other arithmetic  1.28 us (2%)
    pallas_call x1, Pallas kernels, on_device(): pl.pallas_call(kernel, out_shape=(jax.ShapeDtypeStruct((1, FRAMES), f32),...  67.1 us
    unnamed x1, local copies, waits for them, and re-layouts  1.47 us

profile of v4, /device:TPU:32, one launch (start us, length us, event | category | flops | bytes accessed | tf_op | source)
XLA Modules:
  0.0 71.7 jit_solution(15185837171925066304)
XLA Ops:
  0.6 1.3 %reshape.21.ids_ref = s32[1,768]{1,0:T(1,128)} reshape(s32[768]{0:T(1024)} %param.12) | data formatting | bytes 6144 | tf_op jit(solution)/shard_map/reshape | solution.py:516
  1.9 67.1 %topic_step.1 = (f32[1,768]{1,0:T(1,128)}, f32[64,256]{1,0:T(8,128)}) custom-call(f32[1,256]{1,0:T(1,128)} %bitcast.3, f32[1,256]{1,0:T(1,128)} %bitcast.4, s32[1,768]{1,0:T(1,128)} %reshape.21.ids_ref, s32[1,256]{1,0:T(1,128)} %bitcast.5, bf16[256,768]{1,0:T(8,128)(2,1)} %spec_hbm.1, bf16[256,256]{1,0:T(8,128)(2,1)} %enc_hbm.1, f32[256,768]{1,0:T(8,128)} %gauss_hbm.1, ...), custom_call_target="tpu_custom_call" | custom-call | tf_op jit(solution)/shard_map/topic_step/pallas_call | solution.py:493
  69.0 1.3 %reduce = f32[768]{0:T(1024)} reduce(f32[1,768]{1,0:T(1,128)} %get-tuple-element.4, f32[]{:T(128)} %constant), dimensions={0}, to_apply=%get-tuple-element.4.reduce_sub_computation | reduce | bytes 6148 | tf_op jit(solution)/shard_map/topic_step/pallas_call | solution.py:493
  70.3 1.5 %copy.12 = f32[64,256]{1,0:T(8,128)} copy(f32[64,256]{1,0:T(8,128)} %get-tuple-element.9) | data formatting | bytes 131072

commit v5 on v4

--- a/solution.py
+++ b/solution.py
@@ -41,7 +41,7 @@
 def kernel(
     decay_ref, init_ref, ids_ref, boost_ref, spec_hbm, enc_hbm, gauss_hbm, unif_hbm, tmpl_hbm,
     loss_ref, out_ref,
-    spec_ref, tmpl, gbuf, ubuf, encf, grow, cum, normed, nbuf, pbuf, pf, idh, qbuf, st,
+    spec_ref, tmpl, gbuf, ubuf, encf, grow, cum, normed, nbuf, pbuf, pf, idsend, idh, qbuf, st,
     recon, sbuf, rat, grad, w1, a1, c3, r1, r1f, r2, r3,
     load_sem, enc_s, enc_r, q_s, q_r, id_s, id_r, n_s, n_r, p_s, p_r, h_s, h_r, s_s, s_r,
     rs1_s, rs1_r, rs2_s, rs2_r, rs3_s, rs3_r,
@@ -64,7 +64,12 @@
             return tm - 4 * py + 4 * lax.rem(py + step, 4)
         return tm - 16 * pz + 16 * lax.rem(pz + step, 4)
 
-    peers = [(along(axis, step), fq) for axis in range(3) for step in range(1, 4)]
+    pxy = lax.rem(tm, 16)
+
+    def in_plane(step):
+        return tm - pxy + lax.rem(pxy + step, 16)
+
+    peers = [(in_plane(step), fq) for step in range(1, 16)] + [(along(2, step), fq) for step in range(1, 4)]
     peers += [(tm, lax.rem(fq + i, NF)) for i in range(1, NF)]
     for place, other in peers:
         pl.semaphore_signal(
@@ -110,7 +115,9 @@
     log_row = -lost * (1.0 + lost * (1 / 2 + lost * (1 / 3 + lost * (1 / 4 + lost * (1 / 5 + lost * (1 / 6))))))
     log_col = column(log_row)
     decay_col = column(decay_row)
-    ids = ids_ref[...].astype(f32)
+    ids_row = ids_ref[...].reshape(1, FRAMES)
+    ids = ids_row.astype(f32)
+    idsend[...] = ids_row[:, FRAMES - 128:]
     lift = jnp.exp(ids * LOG_GAIN)
     load_x.wait()
     carry = jnp.zeros((BINS, 1), f32)
@@ -134,24 +141,22 @@
     q_col = carry * jnp.exp(log_col * float(FRAMES))
     positions = (px, py, pz)
 
-    def q_copy(axis, step):
-        pos = positions[axis]
-        return remote(
-            qbuf.at[axis, pos], qbuf.at[axis, pos], q_s, q_r.at[axis], along(axis, step), fq)
-
-    def q_send(axis, row):
-        qbuf[axis, positions[axis]] = row
-        for step in range(1, 4):
-            q_copy(axis, step).start()
-
-    def q_take(axis, jump):
-        pos = positions[axis]
-        take(qbuf.at[axis, pl.ds(0, 3)], q_r.at[axis])
+    def q_send(stage, row):
+        pos, count, place = ((pxy, 16, in_plane), (pz, 4, lambda step: along(2, step)))[stage]
+        slot = qbuf.at[16 * stage + pos]
+        slot[...] = row
+        for step in range(1, count):
+            remote(slot, slot, q_s, q_r.at[stage], place(step), fq).start()
+
+    def q_take(stage, jump):
+        pos, count = ((pxy, 16), (pz, 4))[stage]
+        take(qbuf.at[pl.ds(0, count - 1)], q_r.at[stage])
         ahead = jnp.zeros((1, BINS), f32)
         total = jnp.zeros((1, BINS), f32)
-        for j in range(4):
-            ahead = jnp.where(j < pos, jump * ahead + qbuf[axis, j], ahead)
-            total = jump * total + qbuf[axis, j]
+        for j in range(count):
+            row = qbuf[16 * stage + j]
+            ahead = jnp.where(j < pos, jump * ahead + row, ahead)
+            total = jump * total + row
         return ahead, total
 
     q_row = row_of(q_col)
@@ -177,17 +182,12 @@
     def _():
         ready_noise(1)
 
-    entry = jnp.zeros((1, BINS), f32)
-    gain = jnp.ones((1, BINS), f32)
-    for axis in range(3):
-        frames = float(FRAMES * 4 ** axis)
-        ahead, total = q_take(axis, jnp.exp(log_row * frames))
-        if axis < 2:
-            q_send(axis + 1, total)
-        entry += gain * ahead
-        gain = gain * jnp.exp(log_row * (frames * positions[axis].astype(f32)))
-    entry += gain * init_ref[...]
-    id_copy = remote(ids_ref.at[:, pl.ds(FRAMES - 128, 128)], idh, id_s, id_r, nxt, fq)
+    near, total = q_take(0, jnp.exp(log_row * float(FRAMES)))
+    q_send(1, total)
+    far, total = q_take(1, jnp.exp(log_row * float(16 * FRAMES)))
+    entry = near + jnp.exp(log_row * (float(FRAMES) * pxy.astype(f32))) * (
+        far + jnp.exp(log_row * (float(16 * FRAMES) * pz.astype(f32))) * init_ref[...])
+    id_copy = remote(idsend, idh, id_s, id_r, nxt, fq)
 
     @pl.when(tm < TM - 1)
     def _():
@@ -456,7 +456,7 @@
     out_ref[:, 0:128] = c3[3, 0] + r3[2] + r3[4]
     out_ref[:, 128:256] = c3[3, 1] + r3[1] + r3[5]
 
-    sent(qbuf.at[:, pl.ds(0, 3)], q_s)
+    sent(qbuf.at[pl.ds(0, 18)], q_s)
     sent(encf.at[pl.ds(0, 3)], enc_s)
     sent(sbuf.at[pl.ds(0, 3)], s_s)
 
@@ -481,6 +481,11 @@
     sent(tmpl, rs1_s)
     sent(recon, rs2_s)
     sent(pbuf.at[pl.ds(0, 3)], rs3_s)
+
+
+def hand_over(loss_in, grad_in, loss_ref, grad_ref):
+    loss_ref[...] = loss_in[...].reshape(FRAMES)
+    grad_ref[...] = grad_in[...]
 
 
 def on_device(
@@ -502,21 +507,27 @@
             V((BINS, FRAMES), bf16), V((BINS, K * L), bf16), V((2, K, 128), f32), V((2, 2, K, 128), f32), V((NF, K, BINS), bf16),
             V((BINS, FRAMES), f32), V((BINS, FRAMES), f32), V((TILES, BINS, 128), bf16),
             V((2, NF, BINS, 128), bf16), V((TILES + 1, K, 128), bf16), V((TILES + 1, K, 128), f32),
-            V((1, 128), jnp.int32), V((3, 4, 1, BINS), f32), V((K * L, FRAMES), bf16),
+            V((1, 128), jnp.int32), V((1, 128), jnp.int32), V((20, 1, BINS), f32), V((K * L, FRAMES), bf16),
             V((BINS, FRAMES), f32), V((NF, 8, FRAMES), f32), V((BINS, FRAMES), bf16),
             V((4, 2, 4, 4, 64, 128), f32), V((4, 2, 6, 2, 64, 128), bf16), V((4, 2, 4, 64, 128), f32),
             V((4, 2, 64, 128), f32), V((4, 2, 6, 2, 64, 128), bf16), V((4, 2, 2, 2, 64, 128), f32), V((4, 2, 6, 32, 128), f32), V((6, 64, 128), f32),
-            dma((7,)), dma, dma, dma, dma((3,)), dma, dma, dma, dma((2,)), dma, dma, dma, dma, dma, dma,
+            dma((7,)), dma, dma, dma, dma((2,)), dma, dma, dma, dma((2,)), dma, dma, dma, dma, dma, dma,
             dma, dma((4, 2)), dma, dma((4, 2)), dma, dma((3,)),
         ],
         compiler_params=pltpu.CompilerParams(
             collective_id=0, has_side_effects=True, vmem_limit_bytes=56 * 1024 * 1024),
         name="topic_step",
     )(
-        decay_rate.reshape(1, BINS), init_state.reshape(1, BINS), clip_ids.reshape(1, FRAMES),
+        decay_rate.reshape(1, BINS), init_state.reshape(1, BINS), clip_ids,
         boost_count.reshape(1, K), spectrum, encoder, gauss_noise, uniform_noise, templates,
     )
-    return loss.reshape(FRAMES), grad
+    return pl.pallas_call(
+        hand_over,
+        out_shape=(jax.ShapeDtypeStruct((FRAMES,), f32), jax.ShapeDtypeStruct((K * L // TM, BINS), f32)),
+        in_specs=[vmem] * 2,
+        out_specs=(vmem, vmem),
+        name="hand_over",
+    )(loss, grad)
 
 
 def solution(mesh):

time: 72.4 us -> 68.8 us (0.950)
  local copies, waits for them, and re-layouts: 2.74 us -> 0 us
  other arithmetic: 1.28 us -> 0 us
  Pallas kernels: 67.1 us -> 68 us
    pallas_call x0 -> x1, Pallas kernels: none -> 1.48 us  [on_device(): pl.pallas_call(hand_over, out_shape=(jax.ShapeDtypeStruct((FRAMES,), f32)...]
    unnamed x1 -> x0, local copies, waits for them, and re-layouts: 1.47 us -> none
    pallas_call x1 -> x0, other arithmetic: 1.28 us -> none  [on_device(): pl.pallas_call(kernel, out_shape=(jax.ShapeDtypeStruct((1, FRAMES), f32),...]
    reshape x1 -> x0, local copies, waits for them, and re-layouts: 1.27 us -> none  [on_device(): clip_ids.reshape(1, FRAMES)]
where the time goes in v5:
time: 68.8 us; the launch traced here: 68.7 us
  Pallas kernels  68 us (99%)
    pallas_call x1, Pallas kernels, on_device(): pl.pallas_call(kernel, out_shape=(jax.ShapeDtypeStruct((1, FRAMES), f32),...  66.5 us
    pallas_call x1, Pallas kernels, on_device(): pl.pallas_call(hand_over, out_shape=(jax.ShapeDtypeStruct((FRAMES,), f32)...  1.48 us

profile of v5, /device:TPU:32, one launch (start us, length us, event | category | flops | bytes accessed | tf_op | source)
XLA Modules:
  0.0 68.7 jit_solution(7675678682730125412)
XLA Ops:
  0.6 66.5 %topic_step.1 = (f32[1,768]{1,0:T(1,128)}, f32[64,256]{1,0:T(8,128)}) custom-call(f32[1,256]{1,0:T(1,128)} %bitcast.3, f32[1,256]{1,0:T(1,128)} %bitcast.4, s32[768]{0:T(1024)} %ids_ref.1, s32[1,256]{1,0:T(1,128)} %bitcast.5, bf16[256,768]{1,0:T(8,128)(2,1)} %spec_hbm.1, bf16[256,256]{1,0:T(8,128)(2,1)} %enc_hbm.1, f32[256,768]{1,0:T(8,128)} %gauss_hbm.1, ...), custom_call_target="tpu_custom_call" | custom-call | tf_op jit(solution)/shard_map/topic_step/pallas_call | solution.py:498
  67.2 1.5 %hand_over.1 = (f32[768]{0:T(1024)}, f32[64,256]{1,0:T(8,128)}) custom-call(f32[1,768]{1,0:T(1,128)} %get-tuple-element.4.loss_in, f32[64,256]{1,0:T(8,128)} %get-tuple-element.5.grad_in), custom_call_target="tpu_custom_call" | custom-call | tf_op jit(solution)/shard_map/hand_over/pallas_call | solution.py:524

commit v6 on v5

--- a/solution.py
+++ b/solution.py
@@ -42,8 +42,8 @@
     decay_ref, init_ref, ids_ref, boost_ref, spec_hbm, enc_hbm, gauss_hbm, unif_hbm, tmpl_hbm,
     loss_ref, out_ref,
     spec_ref, tmpl, gbuf, ubuf, encf, grow, cum, normed, nbuf, pbuf, pf, idsend, idh, qbuf, st,
-    recon, sbuf, rat, grad, w1, a1, c3, r1, r1f, r2, r3,
-    load_sem, enc_s, enc_r, q_s, q_r, id_s, id_r, n_s, n_r, p_s, p_r, h_s, h_r, s_s, s_r,
+    tbuf, sums, sbuf, rat, grad, w1, a1, c3, r1, r1f, r2, r3,
+    load_sem, t_s, t_r, enc_s, enc_r, q_s, q_r, id_s, id_r, n_s, n_r, p_s, p_r, h_s, h_r, s_s, s_r,
     rs1_s, rs1_r, rs2_s, rs2_r, rs3_s, rs3_r,
 ):
     tm = lax.axis_index("tm")
@@ -80,7 +80,7 @@
     load_e = pltpu.make_async_copy(enc_hbm, encf.at[fq], load_sem.at[6])
     load_e.start()
     first = zlo * 3 + core * 2
-    load_t = pltpu.make_async_copy(tmpl_hbm, tmpl, load_sem.at[0])
+    load_t = pltpu.make_async_copy(tmpl_hbm, tmpl.at[pl.ds(0, BINS)], load_sem.at[0])
 
     def tile_loads(slot):
         cols = pl.ds(pl.multiple_of((first + slot) * 128, 128), 128)
@@ -169,6 +169,13 @@
     load_e.wait()
     for i in range(1, NF):
         enc_copy(i).start()
+    load_t.wait()
+    ones = jnp.ones((8, BINS), bf16)
+    tbuf[fq, :, 0:K * L] = jnp.dot(ones, tmpl[0:BINS, :], preferred_element_type=f32)[0:1]
+    tbuf[fq, :, K * L:] = jnp.dot(ones, spec_ref[...], preferred_element_type=f32)[0:1]
+    for i in range(1, NF):
+        remote(tbuf.at[fq], tbuf.at[fq], t_s, t_r, tm, lax.rem(fq + i, NF)).start()
+
     boost = column(boost_ref[...].astype(f32))
 
     def ready_noise(slot):
@@ -184,6 +191,16 @@
 
     near, total = q_take(0, jnp.exp(log_row * float(FRAMES)))
     q_send(1, total)
+    take(tbuf.at[pl.ds(0, 3)], t_r)
+    whole = tbuf[0] + tbuf[1] + tbuf[2] + tbuf[3]
+    sums[1:2] = whole[:, K * L:]
+    whole = whole[:, 0:K * L]
+    hi = whole.astype(bf16).astype(f32)
+    mid = (whole - hi).astype(bf16).astype(f32)
+    low = whole - hi - mid
+    place = lax.broadcasted_iota(jnp.int32, (16, K * L), 0)
+    tmpl[BINS:, :] = jnp.where(
+        place == 0, hi, jnp.where(place == 1, mid, jnp.where(place == 2, low, 0.0))).astype(bf16)
     far, total = q_take(1, jnp.exp(log_row * float(16 * FRAMES)))
     entry = near + jnp.exp(log_row * (float(FRAMES) * pxy.astype(f32))) * (
         far + jnp.exp(log_row * (float(16 * FRAMES) * pz.astype(f32))) * init_ref[...])
@@ -305,29 +322,22 @@
 
     lax.fori_loop(0, K, build_row, 0, unroll=16)
 
-    load_t.wait()
+    scale = F * K / TIME
     for b in range(3):
         span = slice(b * 256, b * 256 + 256)
         rec = jnp.dot(tmpl[...], st[:, span], preferred_element_type=f32)
+        recon_sum = rec[BINS:BINS + 1] + rec[BINS + 1:BINS + 2] + rec[BINS + 2:BINS + 3]
+        rec = rec[0:BINS]
         x = spec_ref[:, span].astype(f32)
-        recon[:, span] = x / rec
-        sbuf[fq, 0:1, span] = jnp.sum(rec, axis=0, keepdims=True)
-        sbuf[fq, 1:2, span] = jnp.sum(x, axis=0, keepdims=True)
-        sbuf[fq, 2:3, span] = jnp.sum(x * jnp.log(rec), axis=0, keepdims=True)
+        rat[:, span] = (scale / recon_sum - (scale / sums[1:2, span]) * (x / rec)).astype(bf16)
+        sums[0:1, span] = recon_sum
+        sbuf[fq, :, span] = jnp.sum(x * jnp.log(rec), axis=0, keepdims=True)
 
     def s_copy(i):
         return remote(sbuf.at[fq], sbuf.at[fq], s_s, s_r, tm, lax.rem(fq + i, NF))
 
     for i in range(1, NF):
         s_copy(i).start()
-    take(sbuf.at[pl.ds(0, 3)], s_r)
-    sums = sbuf[0, 0:3, :] + sbuf[1, 0:3, :] + sbuf[2, 0:3, :] + sbuf[3, 0:3, :]
-    recon_sum, spec_sum, log_sum = sums[0:1], sums[1:2], sums[2:3]
-    loss_ref[...] = jnp.log(recon_sum) - log_sum / spec_sum
-    scale = F * K / TIME
-    plain = scale / recon_sum
-    part = scale / spec_sum
-    rat[...] = (plain - part * recon[...]).astype(bf16)
 
     def gradient(n):
         z = lax.rem(pz + ORDER[n], 4)
@@ -452,6 +462,9 @@
     relay2(3)
     done2(2)
     done2(3)
+    take(sbuf.at[pl.ds(0, 3)], s_r)
+    log_sum = sbuf[0] + sbuf[1] + sbuf[2] + sbuf[3]
+    loss_ref[...] = jnp.log(sums[0:1]) - log_sum / sums[1:2]
     take(r3.at[pl.ds(0, 4)], rs3_r.at[2])
     out_ref[:, 0:128] = c3[3, 0] + r3[2] + r3[4]
     out_ref[:, 128:256] = c3[3, 1] + r3[1] + r3[5]
@@ -459,6 +472,7 @@
     sent(qbuf.at[pl.ds(0, 18)], q_s)
     sent(encf.at[pl.ds(0, 3)], enc_s)
     sent(sbuf.at[pl.ds(0, 3)], s_s)
+    sent(tbuf.at[pl.ds(0, 3)], t_s)
 
     @pl.when(tm < TM - 1)
     def _():
@@ -478,8 +492,8 @@
     def _():
         sent(pbuf.at[pl.ds(0, 4)], h_s)
 
-    sent(tmpl, rs1_s)
-    sent(recon, rs2_s)
+    sent(tmpl.at[pl.ds(0, BINS)], rs1_s)
+    sent(grow, rs2_s)
     sent(pbuf.at[pl.ds(0, 3)], rs3_s)
 
 
@@ -504,14 +518,14 @@
         in_specs=[vmem] * 4 + [hbm] * 5,
         out_specs=(vmem, vmem),
         scratch_shapes=[
-            V((BINS, FRAMES), bf16), V((BINS, K * L), bf16), V((2, K, 128), f32), V((2, 2, K, 128), f32), V((NF, K, BINS), bf16),
+            V((BINS, FRAMES), bf16), V((BINS + 16, K * L), bf16), V((2, K, 128), f32), V((2, 2, K, 128), f32), V((NF, K, BINS), bf16),
             V((BINS, FRAMES), f32), V((BINS, FRAMES), f32), V((TILES, BINS, 128), bf16),
             V((2, NF, BINS, 128), bf16), V((TILES + 1, K, 128), bf16), V((TILES + 1, K, 128), f32),
             V((1, 128), jnp.int32), V((1, 128), jnp.int32), V((20, 1, BINS), f32), V((K * L, FRAMES), bf16),
-            V((BINS, FRAMES), f32), V((NF, 8, FRAMES), f32), V((BINS, FRAMES), bf16),
+            V((NF, 1, K * L + FRAMES), f32), V((2, FRAMES), f32), V((NF, 1, FRAMES), f32), V((BINS, FRAMES), bf16),
             V((4, 2, 4, 4, 64, 128), f32), V((4, 2, 6, 2, 64, 128), bf16), V((4, 2, 4, 64, 128), f32),
             V((4, 2, 64, 128), f32), V((4, 2, 6, 2, 64, 128), bf16), V((4, 2, 2, 2, 64, 128), f32), V((4, 2, 6, 32, 128), f32), V((6, 64, 128), f32),
-            dma((7,)), dma, dma, dma, dma((2,)), dma, dma, dma, dma((2,)), dma, dma, dma, dma, dma, dma,
+            dma((7,)), dma, dma, dma, dma, dma, dma((2,)), dma, dma, dma, dma((2,)), dma, dma, dma, dma, dma, dma,
             dma, dma((4, 2)), dma, dma((4, 2)), dma, dma((3,)),
         ],
         compiler_params=pltpu.CompilerParams(

time: 68.8 us -> 67.8 us (0.985)
  the two profiles are of different devices: /device:TPU:32 before, /device:TPU:8 now
where the time goes in v6:
time: 67.8 us; the launch traced here: 67.6 us
  Pallas kernels  67 us (99%)
    pallas_call x1, Pallas kernels, on_device(): pl.pallas_call(kernel, out_shape=(jax.ShapeDtypeStruct((1, FRAMES), f32),...  65.5 us
    pallas_call x1, Pallas kernels, on_device(): pl.pallas_call(hand_over, out_shape=(jax.ShapeDtypeStruct((FRAMES,), f32)...  1.48 us

profile of v6, /device:TPU:8, one launch (start us, length us, event | category | flops | bytes accessed | tf_op | source)
XLA Modules:
  0.0 67.6 jit_solution(5356835495138037639)
XLA Ops:
  0.6 65.5 %topic_step.1 = (f32[1,768]{1,0:T(1,128)}, f32[64,256]{1,0:T(8,128)}) custom-call(f32[1,256]{1,0:T(1,128)} %bitcast.3, f32[1,256]{1,0:T(1,128)} %bitcast.4, s32[768]{0:T(1024)} %ids_ref.1, s32[1,256]{1,0:T(1,128)} %bitcast.5, bf16[256,768]{1,0:T(8,128)(2,1)} %spec_hbm.1, bf16[256,256]{1,0:T(8,128)(2,1)} %enc_hbm.1, f32[256,768]{1,0:T(8,128)} %gauss_hbm.1, ...), custom_call_target="tpu_custom_call" | custom-call | tf_op jit(solution)/shard_map/topic_step/pallas_call | solution.py:512
  66.1 1.5 %hand_over.1 = (f32[768]{0:T(1024)}, f32[64,256]{1,0:T(8,128)}) custom-call(f32[1,768]{1,0:T(1,128)} %get-tuple-element.4.loss_in, f32[64,256]{1,0:T(8,128)} %get-tuple-element.5.grad_in), custom_call_target="tpu_custom_call" | custom-call | tf_op jit(solution)/shard_map/hand_over/pallas_call | solution.py:538

commit v7 on v6

--- a/solution.py
+++ b/solution.py
@@ -41,7 +41,7 @@
 def kernel(
     decay_ref, init_ref, ids_ref, boost_ref, spec_hbm, enc_hbm, gauss_hbm, unif_hbm, tmpl_hbm,
     loss_ref, out_ref,
-    spec_ref, tmpl, gbuf, ubuf, encf, grow, cum, normed, nbuf, pbuf, pf, idsend, idh, qbuf, st,
+    spec_ref, tmpl, gbuf, ubuf, encf, grow, cum, normed, nbuf, pbuf, pf, hsend, hbuf, idsend, idh, qbuf, st,
     tbuf, sums, sbuf, rat, grad, w1, a1, c3, r1, r1f, r2, r3,
     load_sem, t_s, t_r, enc_s, enc_r, q_s, q_r, id_s, id_r, n_s, n_r, p_s, p_r, h_s, h_r, s_s, s_r,
     rs1_s, rs1_r, rs2_s, rs2_r, rs3_s, rs3_r,
@@ -50,6 +50,8 @@
     fq = lax.axis_index("freq")
     core = lax.rem(fq, 2)
     zlo = fq // 2
+    mate = fq + 1 - 2 * core
+    cross = lax.rem(fq + 2, NF)
     barrier = pltpu.get_barrier_semaphore()
     nxt = lax.rem(tm + 1, TM)
 
@@ -163,12 +165,10 @@
     pl.semaphore_wait(barrier, len(peers))
     q_send(0, q_row)
 
-    def enc_copy(i):
-        return remote(encf.at[fq], encf.at[fq], enc_s, enc_r, tm, lax.rem(fq + i, NF))
-
     load_e.wait()
-    for i in range(1, NF):
-        enc_copy(i).start()
+    remote(encf.at[fq], encf.at[fq], enc_s, enc_r.at[0], tm, cross).start()
+    remote(encf.at[fq], encf.at[fq], enc_s, enc_r.at[1], tm, mate).start()
+
     load_t.wait()
     ones = jnp.ones((8, BINS), bf16)
     tbuf[fq, :, 0:K * L] = jnp.dot(ones, tmpl[0:BINS, :], preferred_element_type=f32)[0:1]
@@ -191,6 +191,8 @@
 
     near, total = q_take(0, jnp.exp(log_row * float(FRAMES)))
     q_send(1, total)
+    take(encf.at[0], enc_r.at[0])
+    remote(encf.at[cross], encf.at[cross], enc_s, enc_r.at[1], tm, mate).start()
     take(tbuf.at[pl.ds(0, 3)], t_r)
     whole = tbuf[0] + tbuf[1] + tbuf[2] + tbuf[3]
     sums[1:2] = whole[:, K * L:]
@@ -230,13 +232,13 @@
         def _(t=t):
             nbuf[SLOT[t], fq] = normed[t]
 
-    take(encf.at[pl.ds(0, 3)], enc_r)
-
-    def p_copy(t, i):
-        return remote(pbuf.at[1 + t], pbuf.at[1 + t], p_s, p_r, tm, lax.rem(fq + i, NF))
+    take(encf.at[pl.ds(0, 2)], enc_r.at[1])
+
+    def p_copy(t, sem, to):
+        return remote(pbuf.at[1 + t], pbuf.at[1 + t], p_s, p_r.at[sem], tm, to)
 
     def halo_copy(q):
-        return remote(pbuf.at[TILES], pbuf.at[0], h_s, h_r, nxt, q)
+        return remote(hsend, hbuf, h_s, h_r, nxt, q)
 
     def sample(slot):
         take(nbuf.at[slot, pl.ds(0, 3)], n_r.at[slot])
@@ -252,33 +254,37 @@
         total = jnp.sum(draw, axis=0, keepdims=True)
         pbuf[1 + first + slot] = (draw / total).astype(bf16)
 
+    def spread(slot):
+        p_copy(first + slot, slot, cross).start()
+        p_copy(first + slot, 2, mate).start()
+
+    def forward(slot):
+        take(pbuf.at[0], p_r.at[slot])
+        p_copy((1 - zlo) * 3 + core * 2 + slot, 2, mate).start()
+
     sample(0)
-    for t in range(TILES):
-        if SLOT[t] == 0:
-            @pl.when(fq == OWNER[t])
-            def _(t=t):
-                for i in range(1, NF):
-                    p_copy(t, i).start()
+    spread(0)
 
     @pl.when((fq == NF - 1) & (tm < TM - 1))
     def _():
+        hsend[...] = jnp.transpose(pbuf[TILES].astype(f32))[128 - L:].astype(bf16)
         for q in range(NF):
             halo_copy(q).start()
 
     @pl.when(core == 0)
     def _():
         sample(1)
-
-    for t in range(TILES):
-        if SLOT[t] == 1:
-            @pl.when(fq == OWNER[t])
-            def _(t=t):
-                for i in range(1, NF):
-                    p_copy(t, i).start()
+        spread(1)
+
+    forward(0)
+
+    @pl.when(core == 0)
+    def _():
+        forward(1)
 
     @pl.when(tm == 0)
     def _():
-        pbuf[0] = jnp.zeros((K, 128), bf16)
+        hbuf[...] = jnp.zeros((L, K), bf16)
         idh[...] = jnp.full((1, 128), -1, jnp.int32)
 
     @pl.when(tm > 0)
@@ -288,11 +294,11 @@
 
     @pl.when(core == 0)
     def _():
-        take(pbuf.at[pl.ds(0, 4)], p_r)
+        take(pbuf.at[pl.ds(0, 2)], p_r.at[2])
 
     @pl.when(core == 1)
     def _():
-        take(pbuf.at[pl.ds(0, 5)], p_r)
+        take(pbuf.at[pl.ds(0, 4)], p_r.at[2])
 
     lane = lax.broadcasted_iota(jnp.int32, (L, 128), 1)
     lag = lax.broadcasted_iota(jnp.int32, (L, 128), 0)
@@ -308,7 +314,8 @@
         source = jnp.where(head, rolled[t], rolled[t + 1])
         keep.append(source == jnp.broadcast_to(id_rows[t + 1], (L, 128)))
 
-    for t in range(TILES + 1):
+    pf[0] = jnp.transpose(jnp.concatenate([jnp.zeros((128 - L, K), f32), hbuf[...].astype(f32)], axis=0))
+    for t in range(1, TILES + 1):
         pf[t] = pbuf[t].astype(f32)
 
     def build_row(k, carry):
@@ -490,7 +497,7 @@
 
     @pl.when((fq == NF - 1) & (tm < TM - 1))
     def _():
-        sent(pbuf.at[pl.ds(0, 4)], h_s)
+        sent(encf.at[0, pl.ds(0, 64)], h_s)
 
     sent(tmpl.at[pl.ds(0, BINS)], rs1_s)
     sent(grow, rs2_s)
@@ -521,11 +528,11 @@
             V((BINS, FRAMES), bf16), V((BINS + 16, K * L), bf16), V((2, K, 128), f32), V((2, 2, K, 128), f32), V((NF, K, BINS), bf16),
             V((BINS, FRAMES), f32), V((BINS, FRAMES), f32), V((TILES, BINS, 128), bf16),
             V((2, NF, BINS, 128), bf16), V((TILES + 1, K, 128), bf16), V((TILES + 1, K, 128), f32),
-            V((1, 128), jnp.int32), V((1, 128), jnp.int32), V((20, 1, BINS), f32), V((K * L, FRAMES), bf16),
+            V((L, K), bf16), V((L, K), bf16), V((1, 128), jnp.int32), V((1, 128), jnp.int32), V((20, 1, BINS), f32), V((K * L, FRAMES), bf16),
             V((NF, 1, K * L + FRAMES), f32), V((2, FRAMES), f32), V((NF, 1, FRAMES), f32), V((BINS, FRAMES), bf16),
             V((4, 2, 4, 4, 64, 128), f32), V((4, 2, 6, 2, 64, 128), bf16), V((4, 2, 4, 64, 128), f32),
             V((4, 2, 64, 128), f32), V((4, 2, 6, 2, 64, 128), bf16), V((4, 2, 2, 2, 64, 128), f32), V((4, 2, 6, 32, 128), f32), V((6, 64, 128), f32),
-            dma((7,)), dma, dma, dma, dma, dma, dma((2,)), dma, dma, dma, dma((2,)), dma, dma, dma, dma, dma, dma,
+            dma((7,)), dma, dma, dma, dma((2,)), dma, dma((2,)), dma, dma, dma, dma((2,)), dma, dma((3,)), dma, dma, dma, dma,
             dma, dma((4, 2)), dma, dma((4, 2)), dma, dma((3,)),
         ],
         compiler_params=pltpu.CompilerParams(

time: 67.8 us -> 63.9 us (0.942)
  the two profiles are of different devices: /device:TPU:8 before, /device:TPU:32 now
where the time goes in v7:
time: 63.9 us; the launch traced here: 63.5 us
  Pallas kernels  62.9 us (98%)
  between operations  0.64 us (1%)
    pallas_call x1, Pallas kernels, on_device(): pl.pallas_call(kernel, out_shape=(jax.ShapeDtypeStruct((1, FRAMES), f32),...  61.4 us
    pallas_call x1, Pallas kernels, on_device(): pl.pallas_call(hand_over, out_shape=(jax.ShapeDtypeStruct((FRAMES,), f32)...  1.48 us

profile of v7, /device:TPU:32, one launch (start us, length us, event | category | flops | bytes accessed | tf_op | source)
XLA Modules:
  0.0 63.5 jit_solution(12882760010816774341)
XLA Ops:
  0.6 61.4 %topic_step.1 = (f32[1,768]{1,0:T(1,128)}, f32[64,256]{1,0:T(8,128)}) custom-call(f32[1,256]{1,0:T(1,128)} %bitcast.3, f32[1,256]{1,0:T(1,128)} %bitcast.4, s32[768]{0:T(1024)} %ids_ref.1, s32[1,256]{1,0:T(1,128)} %bitcast.5, bf16[256,768]{1,0:T(8,128)(2,1)} %spec_hbm.1, bf16[256,256]{1,0:T(8,128)(2,1)} %enc_hbm.1, f32[256,768]{1,0:T(8,128)} %gauss_hbm.1, ...), custom_call_target="tpu_custom_call" | custom-call | tf_op jit(solution)/shard_map/topic_step/pallas_call | solution.py:519
  62.1 1.5 %hand_over.1 = (f32[768]{0:T(1024)}, f32[64,256]{1,0:T(8,128)}) custom-call(f32[1,768]{1,0:T(1,128)} %get-tuple-element.4.loss_in, f32[64,256]{1,0:T(8,128)} %get-tuple-element.5.grad_in), custom_call_target="tpu_custom_call" | custom-call | tf_op jit(solution)/shard_map/hand_over/pallas_call | solution.py:545

commit v8 on v7

--- a/solution.py
+++ b/solution.py
@@ -18,8 +18,6 @@
 f32 = jnp.float32
 bf16 = jnp.bfloat16
 LOG_GAIN = 0.22314355131420976
-OWNER = (0, 0, 1, 2, 2, 3)
-SLOT = (0, 1, 0, 0, 1, 0)
 ORDER = (2, 1, 3, 0)
 
 
@@ -213,24 +211,30 @@
         id_copy.start()
 
     entry_col = column(entry)
-    for t in range(TILES):
-        span = slice(t * 128, t * 128 + 128)
-        drop = jnp.exp(ids[:, span] * (-LOG_GAIN))
+    def normalise(t):
+        span = pl.ds(pl.multiple_of(t * 128, 128), 128)
+        drop = jnp.exp(ids_ref[span].reshape(1, 128).astype(f32) * (-LOG_GAIN))
         smooth = grow[:, span] * (entry_col + cum[:, span]) * drop
         normed[t] = (spec_ref[:, span].astype(f32) * lax.rsqrt(smooth + 0.1)).astype(bf16)
 
-    def n_copy(t):
-        return remote(
-            normed.at[t], nbuf.at[SLOT[t], fq], n_s, n_r.at[SLOT[t]], tm, OWNER[t])
-
-    for t in (3, 4, 5, 0, 1, 2):
-        @pl.when(fq != OWNER[t])
-        def _(t=t):
-            n_copy(t).start()
-
-        @pl.when(fq == OWNER[t])
-        def _(t=t):
-            nbuf[SLOT[t], fq] = normed[t]
+    def n_copy(t, slot, to):
+        return remote(normed.at[t], nbuf.at[slot, fq], n_s, n_r.at[slot], tm, to)
+
+    for r, slot, owner in ((0, 0, 0), (2, 0, 1), (1, 1, 0)):
+        t = 3 * (1 - zlo) + r
+        normalise(t)
+        n_copy(t, slot, 2 * (1 - zlo) + owner).start()
+    for r, slot, owner in ((0, 0, 0), (2, 0, 1), (1, 1, 0)):
+        t = 3 * zlo + r
+        normalise(t)
+
+        @pl.when(core != owner)
+        def _(t=t, slot=slot):
+            n_copy(t, slot, mate).start()
+
+        @pl.when(core == owner)
+        def _(t=t, slot=slot):
+            nbuf[slot, fq] = normed[t]
 
     take(encf.at[pl.ds(0, 2)], enc_r.at[1])
 
@@ -519,8 +523,8 @@
     loss, grad = pl.pallas_call(
         kernel,
         out_shape=(
-            jax.ShapeDtypeStruct((1, FRAMES), f32),
-            jax.ShapeDtypeStruct((K * L // TM, BINS), f32),
+            V((1, FRAMES), f32),
+            V((K * L // TM, BINS), f32),
         ),
         in_specs=[vmem] * 4 + [hbm] * 5,
         out_specs=(vmem, vmem),

time: 63.9 us -> 63.9 us (level)
  local copies, waits for them, and re-layouts: 0 us -> 1.2 us
  Pallas kernels: 62.9 us -> 61.7 us
    unnamed x0 -> x4, local copies, waits for them, and re-layouts: none -> 1.2 us
    pallas_call x1, Pallas kernels: 61.4 us -> 60.3 us  [on_device(): pl.pallas_call(kernel, out_shape=(V((1, FRAMES), f32), V((K * L // TM, BI...]
where the time goes in v8:
time: 63.9 us; the launch traced here: 63.6 us
  Pallas kernels  61.7 us (97%)
  local copies, waits for them, and re-layouts  1.2 us (2%)
  between operations  0.65 us (1%)
    pallas_call x1, Pallas kernels, on_device(): pl.pallas_call(kernel, out_shape=(V((1, FRAMES), f32), V((K * L // TM, BI...  60.3 us
    pallas_call x1, Pallas kernels, on_device(): pl.pallas_call(hand_over, out_shape=(jax.ShapeDtypeStruct((FRAMES,), f32)...  1.48 us

profile of v8, /device:TPU:32, one launch (start us, length us, event | category | flops | bytes accessed | tf_op | source)
XLA Modules:
  0.0 63.6 jit_solution(2097937860719803420)
XLA Ops:
  0.6 60.3 %topic_step.1 = (f32[1,768]{1,0:T(1,128)S(1)}, f32[64,256]{1,0:T(8,128)S(1)}) custom-call(f32[1,256]{1,0:T(1,128)} %bitcast.3, f32[1,256]{1,0:T(1,128)} %bitcast.4, s32[768]{0:T(1024)} %ids_ref.1, s32[1,256]{1,0:T(1,128)} %bitcast.5, bf16[256,768]{1,0:T(8,128)(2,1)} %spec_hbm.1, bf16[256,256]{1,0:T(8,128)(2,1)} %enc_hbm.1, f32[256,768]{1,0:T(8,128)} %gauss_hbm.1, ...), custom_call_target="tpu_custom_call" | custom-call | tf_op jit(solution)/shard_map/topic_step/pallas_call | solution.py:523
  60.9 0.0 copy-start
  60.9 0.6 copy-done
  61.5 0.0 copy-start.1
  61.5 0.6 copy-done.1
  62.1 1.5 %hand_over.1 = (f32[768]{0:T(1024)}, f32[64,256]{1,0:T(8,128)}) custom-call(f32[1,768]{1,0:T(1,128)} %copy-done.1, f32[64,256]{1,0:T(8,128)} %copy-done), custom_call_target="tpu_custom_call" | custom-call | tf_op jit(solution)/shard_map/hand_over/pallas_call | solution.py:549
Async XLA Ops:
  60.9 0.6 copy-start
  61.5 0.6 copy-start.1

commit v9 on v8

--- a/solution.py
+++ b/solution.py
@@ -18,6 +18,7 @@
 f32 = jnp.float32
 bf16 = jnp.bfloat16
 LOG_GAIN = 0.22314355131420976
+FAR_FIRST = (10, 9, 11, 6, 14, 2, 8, 5, 7, 13, 15, 1, 3, 4, 12)
 ORDER = (2, 1, 3, 0)
 
 
@@ -69,7 +70,7 @@
     def in_plane(step):
         return tm - pxy + lax.rem(pxy + step, 16)
 
-    peers = [(in_plane(step), fq) for step in range(1, 16)] + [(along(2, step), fq) for step in range(1, 4)]
+    peers = [(along(2, step), fq) for step in ORDER[:3]] + [(in_plane(step), fq) for step in FAR_FIRST]
     peers += [(tm, lax.rem(fq + i, NF)) for i in range(1, NF)]
     for place, other in peers:
         pl.semaphore_signal(
@@ -142,10 +143,10 @@
     positions = (px, py, pz)
 
     def q_send(stage, row):
-        pos, count, place = ((pxy, 16, in_plane), (pz, 4, lambda step: along(2, step)))[stage]
+        pos, steps, place = ((pxy, FAR_FIRST, in_plane), (pz, ORDER[:3], lambda step: along(2, step)))[stage]
         slot = qbuf.at[16 * stage + pos]
         slot[...] = row
-        for step in range(1, count):
+        for step in steps:
             remote(slot, slot, q_s, q_r.at[stage], place(step), fq).start()
 
     def q_take(stage, jump):

time: 63.9 us -> 63.7 us (level)
  no operation moved by 1% of the time
where the time goes in v9:
time: 63.7 us; the launch traced here: 63.6 us
  Pallas kernels  61.7 us (97%)
  local copies, waits for them, and re-layouts  1.2 us (2%)
  between operations  0.65 us (1%)
    pallas_call x1, Pallas kernels, on_device(): pl.pallas_call(kernel, out_shape=(V((1, FRAMES), f32), V((K * L // TM, BI...  60.2 us
    pallas_call x1, Pallas kernels, on_device(): pl.pallas_call(hand_over, out_shape=(jax.ShapeDtypeStruct((FRAMES,), f32)...  1.48 us

profile of v9, /device:TPU:32, one launch (start us, length us, event | category | flops | bytes accessed | tf_op | source)
XLA Modules:
  0.0 63.6 jit_solution(1738126258799161811)
XLA Ops:
  0.6 60.2 %topic_step.1 = (f32[1,768]{1,0:T(1,128)S(1)}, f32[64,256]{1,0:T(8,128)S(1)}) custom-call(f32[1,256]{1,0:T(1,128)} %bitcast.3, f32[1,256]{1,0:T(1,128)} %bitcast.4, s32[768]{0:T(1024)} %ids_ref.1, s32[1,256]{1,0:T(1,128)} %bitcast.5, bf16[256,768]{1,0:T(8,128)(2,1)} %spec_hbm.1, bf16[256,256]{1,0:T(8,128)(2,1)} %enc_hbm.1, f32[256,768]{1,0:T(8,128)} %gauss_hbm.1, ...), custom_call_target="tpu_custom_call" | custom-call | tf_op jit(solution)/shard_map/topic_step/pallas_call | solution.py:524
  60.9 0.0 copy-start
  60.9 0.6 copy-done
  61.5 0.0 copy-start.1
  61.5 0.6 copy-done.1
  62.1 1.5 %hand_over.1 = (f32[768]{0:T(1024)}, f32[64,256]{1,0:T(8,128)}) custom-call(f32[1,768]{1,0:T(1,128)} %copy-done.1, f32[64,256]{1,0:T(8,128)} %copy-done), custom_call_target="tpu_custom_call" | custom-call | tf_op jit(solution)/shard_map/hand_over/pallas_call | solution.py:550
Async XLA Ops:
  60.9 0.6 copy-start
  61.5 0.6 copy-start.1
